TPU v7x, 128 devices: a whole 4x4x4 slice. The times are simulated.
128 devices in a mesh: rows: 16 (over z, y), cols: 4 (over x_lo, core), layers: 2 (over x_hi).
Axes of the slice: x: 4 (x_hi: 2, x_lo: 2; x = x_hi * 2 + x_lo), y: 4, z: 4, core: 2. Of those that a mesh axis runs over, the one named last changes fastest.
Arguments:
- term_now: bfloat16 [384, 128, 2048], P('rows', 'layers', 'cols'), may hold values from -6 to 6
- term_prev: bfloat16 [384, 128, 2048], P('rows', 'layers', 'cols'), may hold values from -6 to 6
- cotangent: bfloat16 [384, 128, 2048], P('rows', None, 'cols'), may hold values from -6 to 6
- ham_blocks: bfloat16 [384, 25, 128, 128], P('rows', None, 'layers'), as said below
- block_mask: int32 [384, 25], P('rows'), may hold values from 0 to 1, as said below
- ham_slope: bfloat16 [384, 25, 128, 128], P('rows', None, 'layers'), may hold values from -0.0012207031 to 0.0012207031
- atom_owner: int32 [384, 128], P('rows'), may hold values from 0 to 63, never falling along the last dimension, each value on 1 to 4 neighbouring positions
Outputs:
- term_next: bfloat16 [384, 128, 2048], P('rows', 'layers', 'cols')
- grad_term: bfloat16 [384, 128, 2048], P('rows', 'layers', 'cols')
- forces: float32 [384, 64], P('rows')
Inputs may be any that keep to these rules, and one draw needn't show every extreme that they name: ham_blocks[i, d] is the transpose of ham_blocks[(i + d - 12) mod 384, 24 - d]: H is symmetric. block_mask[i, d] equals block_mask[(i + d - 12) mod 384, 24 - d], and block_mask[i, 12] is 1. Each row of atom_owner never falls; each atom owns 1 to 4 consecutive row orbitals.
All inputs are finite; a program needn't handle non-finite values.
Results may differ from a plain program's by a relative error of at most 0.005.
Values may be sent and summed in bfloat16 or wider, within the bound.
A program may use at most 128 MiB of HBM per device.

v0:
```python
import jax
import jax.numpy as jnp
from jax import lax
from jax.sharding import PartitionSpec as P

APB = 64


def extended_2(cells, sides, width):
    for axis, dim in sides:
        count = lax.axis_size(axis)
        head = lax.slice_in_dim(cells, 0, width, axis=dim)
        tail = lax.slice_in_dim(cells, cells.shape[dim] - width, cells.shape[dim], axis=dim)
        cells = jnp.concatenate(
            [
                lax.ppermute(tail, axis, [(i, (i + 1) % count) for i in range(count)]),
                cells,
                lax.ppermute(head, axis, [((i + 1) % count, i) for i in range(count)]),
            ],
            axis=dim,
        )
    return cells


def from_behind(value, axis, steps):
    count = lax.axis_size(axis)
    pairs = [(source, (source + steps) % count) for source in range(count)]
    return lax.ppermute(value, axis, pairs)


def copy_for_each(shard, axis):
    copies = jnp.broadcast_to(shard, (lax.axis_size(axis), *shard.shape))
    return lax.all_to_all(copies, axis, split_axis=0, concat_axis=0, tiled=True)


def over_copies(shard, axis):
    everything = copy_for_each(shard, axis)
    return jnp.sum(everything, axis=0)


def apply_blocks(ham_blocks, block_mask, extended, rows_dev):

    def apply_advance(offset, summed):
        blocks = lax.dynamic_index_in_dim(ham_blocks, offset, 1, keepdims=False)
        kept_mask = lax.dynamic_index_in_dim(block_mask, offset, 1, keepdims=False)
        masked = blocks * kept_mask.astype(jnp.bfloat16)[:, None, None]
        window = lax.dynamic_slice_in_dim(extended, offset, rows_dev, 0)
        return summed + jnp.einsum(
            "bnm,bnc->bmc", masked, window, preferred_element_type=jnp.float32
        )

    initial = jnp.zeros((rows_dev, ham_blocks.shape[3], extended.shape[2]), jnp.float32)
    return lax.fori_loop(0, ham_blocks.shape[1], apply_advance, initial)


def push_blocks(ham_blocks, block_mask, cotangent, rows_dev):
    reach_rows = (ham_blocks.shape[1] - 1) // 2

    def push_advance(offset, summed):
        blocks = lax.dynamic_index_in_dim(ham_blocks, offset, 1, keepdims=False)
        kept_mask = lax.dynamic_index_in_dim(block_mask, offset, 1, keepdims=False)
        masked = blocks * kept_mask.astype(jnp.bfloat16)[:, None, None]
        sources = jnp.einsum("bnm,bmc->bnc", masked, cotangent, preferred_element_type=jnp.float32)
        window = lax.dynamic_slice_in_dim(summed, offset, rows_dev, 0)
        return lax.dynamic_update_slice_in_dim(summed, window + sources, offset, 0)

    initial = jnp.zeros(
        (rows_dev + 2 * reach_rows, ham_blocks.shape[2], cotangent.shape[2]), jnp.float32
    )
    return lax.fori_loop(0, ham_blocks.shape[1], push_advance, initial)


def force_rows(ham_slope, block_mask, extended, cotangent, rows_dev):

    def force_advance(offset, summed):
        kept_mask = lax.dynamic_index_in_dim(block_mask, offset, 1, keepdims=False).astype(
            jnp.float32
        )
        window = lax.dynamic_slice_in_dim(extended, offset, rows_dev, 0)
        pair_grads = jnp.einsum(
            "bnc,bmc->bnm", window, cotangent, preferred_element_type=jnp.float32
        )
        slope_block = lax.dynamic_index_in_dim(ham_slope, offset, 1, keepdims=False).astype(
            jnp.float32
        )
        return summed + 2.0 * kept_mask[:, None] * jnp.sum(pair_grads * slope_block, axis=1)

    initial = jnp.zeros((rows_dev, cotangent.shape[1]), jnp.float32)
    return lax.fori_loop(0, ham_slope.shape[1], force_advance, initial)


def local(term_now, term_prev, cotangent, ham_blocks, block_mask, ham_slope, atom_owner):
    rows_dev = ham_blocks.shape[0]
    reach_rows = (ham_blocks.shape[1] - 1) // 2
    ext_state = extended_2(term_now, (("rows", 0),), reach_rows)
    forward = lax.psum_scatter(
        apply_blocks(ham_blocks, block_mask, ext_state, rows_dev),
        "layers",
        scatter_dimension=1,
        tiled=True,
    )
    pushed = push_blocks(ham_blocks, block_mask, cotangent, rows_dev)
    from_above = from_behind(pushed[:reach_rows], "rows", -1)
    from_below = from_behind(pushed[rows_dev + reach_rows :], "rows", 1)
    backward = pushed[reach_rows : reach_rows + rows_dev]
    backward = backward.at[:reach_rows].add(from_below)
    backward = backward.at[rows_dev - reach_rows :].add(from_above)
    row_force = force_rows(ham_slope, block_mask, ext_state, cotangent, rows_dev)
    term_next = (2.0 * forward - term_prev.astype(jnp.float32)).astype(jnp.bfloat16)
    grad_term = (2.0 * backward).astype(jnp.bfloat16)
    atom_ids = lax.broadcasted_iota(jnp.int32, (1, 1, APB), 2)
    owners = (atom_owner[:, :, None] == atom_ids).astype(jnp.float32)
    partial_force = jnp.einsum("bm,bma->ba", row_force, owners)
    forces = over_copies(partial_force, ("cols", "layers"))
    return (term_next, grad_term, forces)


def solution(mesh):
    return jax.shard_map(
        local,
        mesh=mesh,
        in_specs=(
            P("rows", "layers", "cols"),
            P("rows", "layers", "cols"),
            P("rows", None, "cols"),
            P("rows", None, "layers", None),
            P("rows", None),
            P("rows", None, "layers", None),
            P("rows", None),
        ),
        out_specs=(P("rows", "layers", "cols"), P("rows", "layers", "cols"), P("rows", None)),
        check_vma=False,
    )
```

profile of v0, /device:TPU:0, one launch (start us, length us, event | category | flops | bytes accessed | tf_op | source)
XLA Modules:
  0.0 436.6 jit_solution(9666371154816386567)
XLA Ops:
  16.6 11.1 %copy.16 = bf16[24,25,64,128]{3,2,0,1:T(8,128)(2,1)} copy(bf16[24,25,64,128]{3,2,1,0:T(8,128)(2,1)} %param.20) | data formatting | bytes 19660800
  31.2 110.3 %while.43 = (s32[]{:T(128)}, f32[48,64,512]{2,1,0:T(8,128)}, bf16[24,25,64,128]{3,2,0,1:T(8,128)(2,1)}, s32[24,25]{0,1:T(8,128)S(1)}, bf16[24,128,512]{2,1,0:T(8,128)(2,1)S(1)}, /*index=5*/s32[]{:T(128)}) while((s32[]{:T(128)}, f32[48,64,512]{2,1,0:T(8,128)}, bf16[24,25,64,128]{3,2,0,1:T(8,128)(2,1)}, s32[24,25]{0,1:T(8,128)S(1)}, ...), condition=%wide.region_4.5_spmd, body=%wide.region_3.4_spmd.sunk | while | flops 202309664 | bytes 9831689 | solution.py:70
  156.4 180.6 %while.44 = (s32[]{:T(128)}, f32[24,128,512]{2,1,0:T(8,128)}, bf16[24,25,64,128]{3,2,0,1:T(8,128)(2,1)}, s32[24,25]{0,1:T(8,128)S(1)}, bf16[48,64,512]{2,1,0:T(8,128)(2,1)}, /*index=5*/s32[]{:T(128)}, s32[]{:T(128)}) while((s32[]{:T(128)}, f32[24,128,512]{2,1,0:T(8,128)}, bf16[24,25,64,128]{3,2,0,1:T(8,128)(2,1)}, ...), condition=%wide.region_1.2_spmd.clone, body=%wide.region_0.1_spmd.clone.sunk | while | flops 204668960 | bytes 14550299 | solution.py:53
  161.8 7.3 %select_add_fusion.4 = f32[24,128,512]{2,1,0:T(8,128)} fusion(f32[24,128,512]{2,1,0:T(8,128)} %get-tuple-element.541, pred[]{:T(512)S(6)} %compare.17, bf16[48,64,512]{2,1,0:T(8,128)(2,1)} %get-tuple-element.551, s32[]{:T(128)} %get-tuple-element.540, bf16[24,25,64,128]{3,2,0,1:T(8,128)(2,1)} %get-tuple-element.549, bf16[24]{0:T(256)(128)(2,1)S(1)} %fusion.42), kind=kOutput, calls=%fused_computation.8.clone.1 | convolution fusion | flops 204668928 | bytes 14550065 | tf_op jit(solution)/shard_map/while/body/eval_jaxpr/bnm,bnc->bmc/dot_general | solution.py:48
  169.1 7.3 %select_add_fusion.4 = f32[24,128,512]{2,1,0:T(8,128)} fusion(f32[24,128,512]{2,1,0:T(8,128)} %get-tuple-element.541, pred[]{:T(512)S(6)} %compare.17, bf16[48,64,512]{2,1,0:T(8,128)(2,1)} %get-tuple-element.551, s32[]{:T(128)} %get-tuple-element.540, bf16[24,25,64,128]{3,2,0,1:T(8,128)(2,1)} %get-tuple-element.549, bf16[24]{0:T(256)(128)(2,1)S(1)} %fusion.42), kind=kOutput, calls=%fused_computation.8.clone.1 | convolution fusion | flops 204668928 | bytes 14550065 | tf_op jit(solution)/shard_map/while/body/eval_jaxpr/bnm,bnc->bmc/dot_general | solution.py:48
  176.4 7.3 %select_add_fusion.4 = f32[24,128,512]{2,1,0:T(8,128)} fusion(f32[24,128,512]{2,1,0:T(8,128)} %get-tuple-element.541, pred[]{:T(512)S(6)} %compare.17, bf16[48,64,512]{2,1,0:T(8,128)(2,1)} %get-tuple-element.551, s32[]{:T(128)} %get-tuple-element.540, bf16[24,25,64,128]{3,2,0,1:T(8,128)(2,1)} %get-tuple-element.549, bf16[24]{0:T(256)(128)(2,1)S(1)} %fusion.42), kind=kOutput, calls=%fused_computation.8.clone.1 | convolution fusion | flops 204668928 | bytes 14550065 | tf_op jit(solution)/shard_map/while/body/eval_jaxpr/bnm,bnc->bmc/dot_general | solution.py:48
  183.7 7.3 %select_add_fusion.4 = f32[24,128,512]{2,1,0:T(8,128)} fusion(f32[24,128,512]{2,1,0:T(8,128)} %get-tuple-element.541, pred[]{:T(512)S(6)} %compare.17, bf16[48,64,512]{2,1,0:T(8,128)(2,1)} %get-tuple-element.551, s32[]{:T(128)} %get-tuple-element.540, bf16[24,25,64,128]{3,2,0,1:T(8,128)(2,1)} %get-tuple-element.549, bf16[24]{0:T(256)(128)(2,1)S(1)} %fusion.42), kind=kOutput, calls=%fused_computation.8.clone.1 | convolution fusion | flops 204668928 | bytes 14550065 | tf_op jit(solution)/shard_map/while/body/eval_jaxpr/bnm,bnc->bmc/dot_general | solution.py:48
  191.0 7.3 %select_add_fusion.4 = f32[24,128,512]{2,1,0:T(8,128)} fusion(f32[24,128,512]{2,1,0:T(8,128)} %get-tuple-element.541, pred[]{:T(512)S(6)} %compare.17, bf16[48,64,512]{2,1,0:T(8,128)(2,1)} %get-tuple-element.551, s32[]{:T(128)} %get-tuple-element.540, bf16[24,25,64,128]{3,2,0,1:T(8,128)(2,1)} %get-tuple-element.549, bf16[24]{0:T(256)(128)(2,1)S(1)} %fusion.42), kind=kOutput, calls=%fused_computation.8.clone.1 | convolution fusion | flops 204668928 | bytes 14550065 | tf_op jit(solution)/shard_map/while/body/eval_jaxpr/bnm,bnc->bmc/dot_general | solution.py:48
  198.3 7.3 %select_add_fusion.4 = f32[24,128,512]{2,1,0:T(8,128)} fusion(f32[24,128,512]{2,1,0:T(8,128)} %get-tuple-element.541, pred[]{:T(512)S(6)} %compare.17, bf16[48,64,512]{2,1,0:T(8,128)(2,1)} %get-tuple-element.551, s32[]{:T(128)} %get-tuple-element.540, bf16[24,25,64,128]{3,2,0,1:T(8,128)(2,1)} %get-tuple-element.549, bf16[24]{0:T(256)(128)(2,1)S(1)} %fusion.42), kind=kOutput, calls=%fused_computation.8.clone.1 | convolution fusion | flops 204668928 | bytes 14550065 | tf_op jit(solution)/shard_map/while/body/eval_jaxpr/bnm,bnc->bmc/dot_general | solution.py:48
  212.9 7.3 %select_add_fusion.4 = f32[24,128,512]{2,1,0:T(8,128)} fusion(f32[24,128,512]{2,1,0:T(8,128)} %get-tuple-element.541, pred[]{:T(512)S(6)} %compare.17, bf16[48,64,512]{2,1,0:T(8,128)(2,1)} %get-tuple-element.551, s32[]{:T(128)} %get-tuple-element.540, bf16[24,25,64,128]{3,2,0,1:T(8,128)(2,1)} %get-tuple-element.549, bf16[24]{0:T(256)(128)(2,1)S(1)} %fusion.42), kind=kOutput, calls=%fused_computation.8.clone.1 | convolution fusion | flops 204668928 | bytes 14550065 | tf_op jit(solution)/shard_map/while/body/eval_jaxpr/bnm,bnc->bmc/dot_general | solution.py:48
  227.5 7.3 %select_add_fusion.4 = f32[24,128,512]{2,1,0:T(8,128)} fusion(f32[24,128,512]{2,1,0:T(8,128)} %get-tuple-element.541, pred[]{:T(512)S(6)} %compare.17, bf16[48,64,512]{2,1,0:T(8,128)(2,1)} %get-tuple-element.551, s32[]{:T(128)} %get-tuple-element.540, bf16[24,25,64,128]{3,2,0,1:T(8,128)(2,1)} %get-tuple-element.549, bf16[24]{0:T(256)(128)(2,1)S(1)} %fusion.42), kind=kOutput, calls=%fused_computation.8.clone.1 | convolution fusion | flops 204668928 | bytes 14550065 | tf_op jit(solution)/shard_map/while/body/eval_jaxpr/bnm,bnc->bmc/dot_general | solution.py:48
  234.8 7.3 %select_add_fusion.4 = f32[24,128,512]{2,1,0:T(8,128)} fusion(f32[24,128,512]{2,1,0:T(8,128)} %get-tuple-element.541, pred[]{:T(512)S(6)} %compare.17, bf16[48,64,512]{2,1,0:T(8,128)(2,1)} %get-tuple-element.551, s32[]{:T(128)} %get-tuple-element.540, bf16[24,25,64,128]{3,2,0,1:T(8,128)(2,1)} %get-tuple-element.549, bf16[24]{0:T(256)(128)(2,1)S(1)} %fusion.42), kind=kOutput, calls=%fused_computation.8.clone.1 | convolution fusion | flops 204668928 | bytes 14550065 | tf_op jit(solution)/shard_map/while/body/eval_jaxpr/bnm,bnc->bmc/dot_general | solution.py:48
  242.1 7.3 %select_add_fusion.4 = f32[24,128,512]{2,1,0:T(8,128)} fusion(f32[24,128,512]{2,1,0:T(8,128)} %get-tuple-element.541, pred[]{:T(512)S(6)} %compare.17, bf16[48,64,512]{2,1,0:T(8,128)(2,1)} %get-tuple-element.551, s32[]{:T(128)} %get-tuple-element.540, bf16[24,25,64,128]{3,2,0,1:T(8,128)(2,1)} %get-tuple-element.549, bf16[24]{0:T(256)(128)(2,1)S(1)} %fusion.42), kind=kOutput, calls=%fused_computation.8.clone.1 | convolution fusion | flops 204668928 | bytes 14550065 | tf_op jit(solution)/shard_map/while/body/eval_jaxpr/bnm,bnc->bmc/dot_general | solution.py:48
  249.4 7.3 %select_add_fusion.4 = f32[24,128,512]{2,1,0:T(8,128)} fusion(f32[24,128,512]{2,1,0:T(8,128)} %get-tuple-element.541, pred[]{:T(512)S(6)} %compare.17, bf16[48,64,512]{2,1,0:T(8,128)(2,1)} %get-tuple-element.551, s32[]{:T(128)} %get-tuple-element.540, bf16[24,25,64,128]{3,2,0,1:T(8,128)(2,1)} %get-tuple-element.549, bf16[24]{0:T(256)(128)(2,1)S(1)} %fusion.42), kind=kOutput, calls=%fused_computation.8.clone.1 | convolution fusion | flops 204668928 | bytes 14550065 | tf_op jit(solution)/shard_map/while/body/eval_jaxpr/bnm,bnc->bmc/dot_general | solution.py:48
  256.7 7.3 %select_add_fusion.4 = f32[24,128,512]{2,1,0:T(8,128)} fusion(f32[24,128,512]{2,1,0:T(8,128)} %get-tuple-element.541, pred[]{:T(512)S(6)} %compare.17, bf16[48,64,512]{2,1,0:T(8,128)(2,1)} %get-tuple-element.551, s32[]{:T(128)} %get-tuple-element.540, bf16[24,25,64,128]{3,2,0,1:T(8,128)(2,1)} %get-tuple-element.549, bf16[24]{0:T(256)(128)(2,1)S(1)} %fusion.42), kind=kOutput, calls=%fused_computation.8.clone.1 | convolution fusion | flops 204668928 | bytes 14550065 | tf_op jit(solution)/shard_map/while/body/eval_jaxpr/bnm,bnc->bmc/dot_general | solution.py:48
  264.0 7.3 %select_add_fusion.4 = f32[24,128,512]{2,1,0:T(8,128)} fusion(f32[24,128,512]{2,1,0:T(8,128)} %get-tuple-element.541, pred[]{:T(512)S(6)} %compare.17, bf16[48,64,512]{2,1,0:T(8,128)(2,1)} %get-tuple-element.551, s32[]{:T(128)} %get-tuple-element.540, bf16[24,25,64,128]{3,2,0,1:T(8,128)(2,1)} %get-tuple-element.549, bf16[24]{0:T(256)(128)(2,1)S(1)} %fusion.42), kind=kOutput, calls=%fused_computation.8.clone.1 | convolution fusion | flops 204668928 | bytes 14550065 | tf_op jit(solution)/shard_map/while/body/eval_jaxpr/bnm,bnc->bmc/dot_general | solution.py:48
  271.3 7.3 %select_add_fusion.4 = f32[24,128,512]{2,1,0:T(8,128)} fusion(f32[24,128,512]{2,1,0:T(8,128)} %get-tuple-element.541, pred[]{:T(512)S(6)} %compare.17, bf16[48,64,512]{2,1,0:T(8,128)(2,1)} %get-tuple-element.551, s32[]{:T(128)} %get-tuple-element.540, bf16[24,25,64,128]{3,2,0,1:T(8,128)(2,1)} %get-tuple-element.549, bf16[24]{0:T(256)(128)(2,1)S(1)} %fusion.42), kind=kOutput, calls=%fused_computation.8.clone.1 | convolution fusion | flops 204668928 | bytes 14550065 | tf_op jit(solution)/shard_map/while/body/eval_jaxpr/bnm,bnc->bmc/dot_general | solution.py:48
  285.9 7.3 %select_add_fusion.4 = f32[24,128,512]{2,1,0:T(8,128)} fusion(f32[24,128,512]{2,1,0:T(8,128)} %get-tuple-element.541, pred[]{:T(512)S(6)} %compare.17, bf16[48,64,512]{2,1,0:T(8,128)(2,1)} %get-tuple-element.551, s32[]{:T(128)} %get-tuple-element.540, bf16[24,25,64,128]{3,2,0,1:T(8,128)(2,1)} %get-tuple-element.549, bf16[24]{0:T(256)(128)(2,1)S(1)} %fusion.42), kind=kOutput, calls=%fused_computation.8.clone.1 | convolution fusion | flops 204668928 | bytes 14550065 | tf_op jit(solution)/shard_map/while/body/eval_jaxpr/bnm,bnc->bmc/dot_general | solution.py:48
  300.5 7.3 %select_add_fusion.4 = f32[24,128,512]{2,1,0:T(8,128)} fusion(f32[24,128,512]{2,1,0:T(8,128)} %get-tuple-element.541, pred[]{:T(512)S(6)} %compare.17, bf16[48,64,512]{2,1,0:T(8,128)(2,1)} %get-tuple-element.551, s32[]{:T(128)} %get-tuple-element.540, bf16[24,25,64,128]{3,2,0,1:T(8,128)(2,1)} %get-tuple-element.549, bf16[24]{0:T(256)(128)(2,1)S(1)} %fusion.42), kind=kOutput, calls=%fused_computation.8.clone.1 | convolution fusion | flops 204668928 | bytes 14550065 | tf_op jit(solution)/shard_map/while/body/eval_jaxpr/bnm,bnc->bmc/dot_general | solution.py:48
  307.8 7.3 %select_add_fusion.4 = f32[24,128,512]{2,1,0:T(8,128)} fusion(f32[24,128,512]{2,1,0:T(8,128)} %get-tuple-element.541, pred[]{:T(512)S(6)} %compare.17, bf16[48,64,512]{2,1,0:T(8,128)(2,1)} %get-tuple-element.551, s32[]{:T(128)} %get-tuple-element.540, bf16[24,25,64,128]{3,2,0,1:T(8,128)(2,1)} %get-tuple-element.549, bf16[24]{0:T(256)(128)(2,1)S(1)} %fusion.42), kind=kOutput, calls=%fused_computation.8.clone.1 | convolution fusion | flops 204668928 | bytes 14550065 | tf_op jit(solution)/shard_map/while/body/eval_jaxpr/bnm,bnc->bmc/dot_general | solution.py:48
  315.1 7.3 %select_add_fusion.4 = f32[24,128,512]{2,1,0:T(8,128)} fusion(f32[24,128,512]{2,1,0:T(8,128)} %get-tuple-element.541, pred[]{:T(512)S(6)} %compare.17, bf16[48,64,512]{2,1,0:T(8,128)(2,1)} %get-tuple-element.551, s32[]{:T(128)} %get-tuple-element.540, bf16[24,25,64,128]{3,2,0,1:T(8,128)(2,1)} %get-tuple-element.549, bf16[24]{0:T(256)(128)(2,1)S(1)} %fusion.42), kind=kOutput, calls=%fused_computation.8.clone.1 | convolution fusion | flops 204668928 | bytes 14550065 | tf_op jit(solution)/shard_map/while/body/eval_jaxpr/bnm,bnc->bmc/dot_general | solution.py:48
  322.4 7.3 %select_add_fusion.4 = f32[24,128,512]{2,1,0:T(8,128)} fusion(f32[24,128,512]{2,1,0:T(8,128)} %get-tuple-element.541, pred[]{:T(512)S(6)} %compare.17, bf16[48,64,512]{2,1,0:T(8,128)(2,1)} %get-tuple-element.551, s32[]{:T(128)} %get-tuple-element.540, bf16[24,25,64,128]{3,2,0,1:T(8,128)(2,1)} %get-tuple-element.549, bf16[24]{0:T(256)(128)(2,1)S(1)} %fusion.42), kind=kOutput, calls=%fused_computation.8.clone.1 | convolution fusion | flops 204668928 | bytes 14550065 | tf_op jit(solution)/shard_map/while/body/eval_jaxpr/bnm,bnc->bmc/dot_general | solution.py:48
  329.7 7.3 %select_add_fusion.4 = f32[24,128,512]{2,1,0:T(8,128)} fusion(f32[24,128,512]{2,1,0:T(8,128)} %get-tuple-element.541, pred[]{:T(512)S(6)} %compare.17, bf16[48,64,512]{2,1,0:T(8,128)(2,1)} %get-tuple-element.551, s32[]{:T(128)} %get-tuple-element.540, bf16[24,25,64,128]{3,2,0,1:T(8,128)(2,1)} %get-tuple-element.549, bf16[24]{0:T(256)(128)(2,1)S(1)} %fusion.42), kind=kOutput, calls=%fused_computation.8.clone.1 | convolution fusion | flops 204668928 | bytes 14550065 | tf_op jit(solution)/shard_map/while/body/eval_jaxpr/bnm,bnc->bmc/dot_general | solution.py:48
  337.0 69.7 %while.45 = (s32[]{:T(128)}, f32[24,128]{1,0:T(8,128)S(1)}, s32[24,25]{0,1:T(8,128)S(1)}, bf16[48,64,512]{2,1,0:T(8,128)(2,1)}, bf16[24,128,512]{2,1,0:T(8,128)(...) while((s32[]{:T(128)}, f32[24,128]{1,0:T(8,128)S(1)}, ...), condition=%wide.region_7.8_spmd.clone, body=%wide.region_5.7_spmd.clone.sunk | while | flops 201922608 | bytes 5162371 | solution.py:89
  (197 shorter events, 265.0 us)
Async XLA Ops:
  7.2 9.4 %copy-start.2 = (s32[24,25]{1,0:T(8,128)S(1)}, s32[24,25]{1,0:T(8,128)}, u32[]{:S(2)}) copy-start(s32[24,25]{1,0:T(8,128)} %param.21) | copy-start | bytes 7204
  7.2 418.5 %reduce-scatter.2.cloned.1.call-start = ((), (), s32[]{:S(2)}) async-start(), calls=%async_computation.2 | async-start | bytes 9437184 | tf_op jit(solution)/shard_map/reduce_scatter | solution.py:96
  9.9 140.9 %collective-permute-start = (bf16[12,64,512]{2,1,0:T(8,128)(2,1)}, bf16[12,64,512]{2,1,0:T(8,128)(2,1)}, u32[]{:S(2)}, u32[]{:S(2)}) collective-permute-start(bf16[12,64,512]{2,1,0:T(8,128)(2,1)} %get-tuple-element.433), channel_id=1, source_target_pairs={{0,8},{8,16},{16,24},{24,32},{32,40},{40,48},{48,56},{56,64},{64,7... | collective-permute-start | bytes 2359304 | tf_op jit(solution)/shard_map/ppermute | solution.py:16
  11.6 141.9 %collective-permute-start.1 = (bf16[12,64,512]{2,1,0:T(8,128)(2,1)}, bf16[12,64,512]{2,1,0:T(8,128)(2,1)}, u32[]{:S(2)}, u32[]{:S(2)}) collective-permute-start(bf16[12,64,512]{2,1,0:T(8,128)(2,1)} %get-tuple-element.432), channel_id=1, source_target_pairs={{8,0},{16,8},{24,16},{32,24},{40,32},{48,40},{56,48},{64,56},{72,6... | collective-permute-start | bytes 2359304 | tf_op jit(solution)/shard_map/ppermute | solution.py:18
  27.7 3.4 copy-start
  145.4 274.6 %collective-permute-start.2 = (f32[12,64,512]{2,1,0:T(8,128)}, f32[12,64,512]{2,1,0:T(8,128)}, u32[]{:S(2)}, u32[]{:S(2)}) collective-permute-start(f32[12,64,512]{2,1,0:T(8,128)} %get-tuple-element.431), channel_id=1, source_target_pairs={{0,8},{8,16},{16,24},{24,32},{32,40},{40,48},{48,56},{56,64},{64,7... | collective-permute-start | bytes 4718600 | tf_op jit(solution)/shard_map/ppermute | solution.py:28
  145.4 276.8 %collective-permute-start.3 = (f32[12,64,512]{2,1,0:T(8,128)}, f32[12,64,512]{2,1,0:T(8,128)}, u32[]{:S(2)}, u32[]{:S(2)}) collective-permute-start(f32[12,64,512]{2,1,0:T(8,128)} %get-tuple-element.430), channel_id=1, source_target_pairs={{0,120},{8,0},{16,8},{24,16},{32,24},{40,32},{48,40},{56,48},{64,5... | collective-permute-start | bytes 4718600 | tf_op jit(solution)/shard_map/ppermute | solution.py:28
  154.7 1.7 copy-start.1
  337.0 69.7 %copy-start.3 = (s32[24,128]{1,0:T(8,128)S(1)}, s32[24,128]{1,0:T(8,128)}, u32[]{:S(2)}) copy-start(s32[24,128]{1,0:T(8,128)} %param.23) | copy-start | bytes 36868
  408.2 9.8 %all-to-all-start = ((f32[8,1,1536]{2,1,0:T(1,128)}), f32[8,1,1536]{2,1,0:T(1,128)S(1)}, u32[]{:S(2)}, u32[]{:S(2)}) async-start(f32[8,1,1536]{2,1,0:T(1,128)} %reshape.90), calls=%async_computation.1 | async-start | bytes 98304 | tf_op jit(solution)/shard_map/all_to_all | solution.py:33
Sparse Core Ops, SparseCore 0:
  337.1 77.4 reduce-scatter.1
where the time goes:
time: 439 us; the launch traced here: 437 us
  matrix products  358 us (82%)
  local copies, waits for them, and re-layouts  30.7 us (7%)
  starting transfers between devices  16.5 us (4%)
  between operations  14.1 us (3%)
  other arithmetic  13.7 us (3%)
    dot_general x25, matrix products, apply_advance(): jnp.einsum('bnm,bnc->bmc', masked, window, preferred_element_type=jnp.flo...  180 us
    dot_general x25, matrix products, push_advance(): jnp.einsum('bnm,bmc->bnc', masked, cotangent, preferred_element_type=jnp....  110 us
    dot_general x25, matrix products, force_advance(): jnp.einsum('bnc,bmc->bnm', window, cotangent, preferred_element_type=jnp....  67 us
    unnamed x14, local copies, waits for them, and re-layouts  16.4 us
  transfers between devices with their start and end apart: 6, of which 1 were waited for; matrix products, arithmetic and copies ran while one was open for 90% of the time, Pallas kernels for 0%

commit v1 on v0

v1 whole, which is shorter than its diff:
```python
import jax
import jax.numpy as jnp
from jax import lax
from jax.experimental import pallas as pl
from jax.experimental.pallas import tpu as pltpu
from jax.sharding import PartitionSpec as P

BF = jnp.bfloat16
F32 = jnp.float32
MESH = pl.DeviceIdType.MESH

ROWS = 24
HALF = 64
ORB = 128
COLS = 512
SLOTS = 25
REACH = 12
STEPS = 6


def remote(src, dst, send_sem, recv_sem, device):
    return pltpu.make_async_remote_copy(
        src_ref=src, dst_ref=dst, send_sem=send_sem, recv_sem=recv_sem,
        device_id=device, device_id_type=MESH,
    )


def kernel(
    mask, owner, tn, tp, cot_h, ham_h, slope_h,
    tno, gro, fo,
    ext, tt, cot, ham, slope, own, xs, xr, bown, bs, br, prev, to, go, rf, fbuf,
    lsem, hsem, osem, hs, hr, xss, xrs, bss, bsr, fs, fr,
):
    row = lax.axis_index("rows")
    col = lax.axis_index("cols")
    lay = lax.axis_index("layers")
    up = {"rows": lax.rem(row + 1, 16)}
    down = {"rows": lax.rem(row + 15, 16)}
    partner = {"layers": 1 - lay}
    me = col * 2 + lay

    def ring(index):
        return {"cols": index // 2, "layers": index % 2}

    barrier = pltpu.get_barrier_semaphore()
    pl.semaphore_signal(barrier, 1, device_id=up, device_id_type=MESH)
    pl.semaphore_signal(barrier, 1, device_id=down, device_id_type=MESH)
    for o in range(1, 8):
        pl.semaphore_signal(
            barrier, 1, device_id=ring(lax.rem(me + o, 8)), device_id_type=MESH
        )

    def load_term():
        return pltpu.make_async_copy(tn, ext.at[pl.ds(REACH, ROWS)], lsem.at[0])

    def load_cot():
        return pltpu.make_async_copy(cot_h, cot, lsem.at[1])

    def load_prev():
        return pltpu.make_async_copy(tp, prev, lsem.at[2])

    def load_blocks(k):
        copies = []
        for side, first in ((0, 10 - 2 * k), (1, 12 + 2 * k)):
            at = pl.ds(first, 2)
            copies.append(pltpu.make_async_copy(ham_h.at[at], ham.at[at], hsem.at[0, side, k]))
            copies.append(
                pltpu.make_async_copy(slope_h.at[at], slope.at[at], hsem.at[1, side, k])
            )
        return copies

    load_term().start()
    for c in load_blocks(0):
        c.start()
    load_cot().start()
    for k in range(1, STEPS):
        for c in load_blocks(k):
            c.start()
    load_prev().start()

    def to_up(k):
        return remote(
            tn.at[pl.ds(22 - 2 * k, 2)], ext.at[pl.ds(10 - 2 * k, 2)],
            hs.at[0, k], hr.at[0, k], up,
        )

    def to_down(k):
        return remote(
            tn.at[pl.ds(2 * k, 2)], ext.at[pl.ds(36 + 2 * k, 2)],
            hs.at[1, k], hr.at[1, k], down,
        )

    pl.semaphore_wait(barrier, 9)
    for k in range(STEPS):
        to_up(k).start()
        to_down(k).start()

    def turn(pair):
        tt[pair] = ext[pl.ds(2 * pair, 2)].reshape(ORB, COLS).T

    load_term().wait()

    def turn_local(p, carry):
        turn(p + 6)
        return carry

    lax.fori_loop(0, 12, turn_local, 0)

    def mask_rows(k, carry):
        for c in load_blocks(k):
            c.wait()
        for first in (10 - 2 * k, 12 + 2 * k):
            for r in range(2):
                i = first + r
                for d in range(SLOTS):
                    kept = jnp.full((HALF, ORB), mask[i, d].astype(F32), F32).astype(BF)
                    ham[i, d] = ham[i, d] * kept
                    slope[i, d] = slope[i, d] * kept
        return carry

    def send_partial(k, side):
        at = pl.ds(10 - 2 * k if side == 0 else 12 + 2 * k, 2)
        return remote(
            xs.at[at], xr.at[at], xss.at[side, k], xrs.at[side, k], partner
        )

    def forward(k, carry):
        to_up(k).wait_recv()
        to_down(k).wait_recv()
        turn(5 - k)
        turn(18 + k)
        for side in range(2):
            pair = 5 - k if side == 0 else 6 + k
            lhs = jnp.concatenate([tt[pair + g] for g in range(13)], axis=1)
            edge = jnp.zeros((HALF, 2 * ORB), BF)
            weights = []
            for r in range(2):
                i = 2 * pair + r
                w = jnp.concatenate(
                    [
                        ham[i].reshape(SLOTS * HALF, ORB),
                        slope[i].reshape(SLOTS * HALF, ORB),
                    ],
                    axis=1,
                )
                weights.append(jnp.concatenate([edge, w] if r else [w, edge], axis=0))
            out = jnp.dot(
                lhs, jnp.concatenate(weights, axis=1), preferred_element_type=F32
            )
            for r in range(2):
                i = 2 * pair + r
                f = out[:, 2 * r * ORB : (2 * r + 1) * ORB].T
                low, high = f[:HALF], f[HALF:]
                own[i] = jnp.where(lay == 0, low, high)
                xs[i] = jnp.where(lay == 0, high, low).astype(BF)
                g = out[:, (2 * r + 1) * ORB : (2 * r + 2) * ORB]
                turned = cot[i].T.astype(F32)
                rf[i] = 2.0 * jnp.sum(turned * g, axis=0, keepdims=True)
            send_partial(k, side).start()
        return carry

    def push_group(g):
        i0, i1 = max(0, 4 * g - 24), min(ROWS - 1, 4 * g + 3)
        parts = []
        for i in range(i0, i1 + 1):
            d0 = 4 * g - i
            lo, hi = max(0, -d0), min(4, SLOTS - d0)
            p = []
            if lo:
                p.append(jnp.zeros((HALF * lo, ORB), BF))
            p.append(ham[i, d0 + lo : d0 + hi].reshape((hi - lo) * HALF, ORB))
            if hi < 4:
                p.append(jnp.zeros((HALF * (4 - hi), ORB), BF))
            parts.append(jnp.concatenate(p, axis=0) if len(p) > 1 else p[0])
        out = jnp.dot(
            jnp.concatenate(parts, axis=1),
            cot[i0 : i1 + 1].reshape((i1 - i0 + 1) * ORB, COLS),
            preferred_element_type=F32,
        )
        return out.reshape(4, HALF, COLS)

    def send_pushed(side, g):
        at = pl.ds(4 * g, 4)
        return remote(
            bs.at[side, at], br.at[1 - side, at], bss.at[side, g], bsr.at[side, g],
            down if side == 0 else up,
        )

    mask_rows(0, 0)
    load_cot().wait()
    forward(0, 0)
    lax.fori_loop(1, STEPS, mask_rows, 0)
    for g in range(3):
        bs[0, 4 * g : 4 * g + 4] = push_group(g).astype(BF)
        bs[1, 4 * g : 4 * g + 4] = push_group(9 + g).astype(BF)
        send_pushed(0, g).start()
        send_pushed(1, g).start()
    lax.fori_loop(1, STEPS, forward, 0)

    atoms = lax.broadcasted_iota(jnp.int32, (HALF, ORB), 0)
    lanes = lax.broadcasted_iota(jnp.int32, (HALF, ORB), 1)

    def gather_atoms(i, total):
        mine = jnp.where(owner[pl.ds(i, 1)] == atoms, rf[i], 0.0)
        summed = jnp.sum(mine, axis=1, keepdims=True)
        return total + jnp.where(lanes == i, summed, 0.0)

    total = lax.fori_loop(0, ROWS, gather_atoms, jnp.zeros((HALF, ORB), F32))
    total = jnp.concatenate([total, jnp.zeros((HALF, ORB), F32)], axis=0).T
    fbuf[me] = total[:ROWS]

    def send_force(o):
        return remote(
            fbuf.at[me], fbuf.at[me], fs.at[o - 1], fr.at[o - 1],
            ring(lax.rem(me + o, 8)),
        )

    def take_force(o):
        slot = lax.rem(me + 8 - o, 8)
        return remote(
            fbuf.at[slot], fbuf.at[slot], fs.at[o - 1], fr.at[o - 1],
            ring(lax.rem(me + o, 8)),
        )

    for o in range(1, 8):
        send_force(o).start()

    for g in range(3, 9):
        bown[4 * (g - 3) : 4 * (g - 2)] = push_group(g)

    for o in range(1, 8):
        take_force(o).wait_recv()
    summed = fbuf[0]
    for s in range(1, 8):
        summed = summed + fbuf[s]
    fo[...] = summed[:, :HALF]

    load_prev().wait()

    def out_term(k, side):
        at = pl.ds(10 - 2 * k if side == 0 else 12 + 2 * k, 2)
        return pltpu.make_async_copy(to.at[at], tno.at[at], osem.at[side, k])

    def out_grad(side, g):
        at = pl.ds(12 * side + 4 * g, 4)
        return pltpu.make_async_copy(go.at[at], gro.at[at], osem.at[side, STEPS + g])

    def finish_term(k, carry):
        for side in range(2):
            at = pl.ds(10 - 2 * k if side == 0 else 12 + 2 * k, 2)
            send_partial(k, side).wait_recv()
            both = own[at] + xr[at].astype(F32)
            to[at] = (2.0 * both - prev[at].astype(F32)).astype(BF)
            out_term(k, side).start()
        return carry

    def finish_grad(g):
        for side in range(2):
            at = pl.ds(12 * side + 4 * g, 4)
            send_pushed(1 - side, g).wait_recv()
            both = bown[at] + br[side, pl.ds(4 * g, 4)].astype(F32)
            go[at] = (2.0 * both).astype(BF)
            out_grad(side, g).start()

    lax.fori_loop(0, 3, finish_term, 0)
    finish_grad(0)
    finish_term(3, 0)
    finish_grad(1)
    finish_term(4, 0)
    finish_grad(2)
    finish_term(5, 0)

    for k in range(STEPS):
        to_up(k).wait_send()
        to_down(k).wait_send()
        for side in range(2):
            send_partial(k, side).wait_send()
            out_term(k, side).wait()
    for g in range(3):
        for side in range(2):
            send_pushed(side, g).wait_send()
            out_grad(side, g).wait()
    for o in range(1, 8):
        send_force(o).wait_send()


def local(term_now, term_prev, cotangent, ham_blocks, block_mask, ham_slope, atom_owner):
    anyspace = pl.BlockSpec(memory_space=pl.ANY)
    dma = pltpu.SemaphoreType.DMA
    block = (ROWS, HALF, COLS)
    return pl.pallas_call(
        kernel,
        out_shape=(
            jax.ShapeDtypeStruct(block, BF),
            jax.ShapeDtypeStruct(block, BF),
            jax.ShapeDtypeStruct((ROWS, HALF), F32),
        ),
        in_specs=[
            pl.BlockSpec(memory_space=pltpu.SMEM),
            pl.BlockSpec(memory_space=pltpu.VMEM),
            anyspace, anyspace, anyspace, anyspace, anyspace,
        ],
        out_specs=(anyspace, anyspace, pl.BlockSpec(memory_space=pltpu.VMEM)),
        scratch_shapes=[
            pltpu.VMEM((ROWS + 2 * REACH, HALF, COLS), BF),
            pltpu.VMEM((24, COLS, ORB), BF),
            pltpu.VMEM((ROWS, ORB, COLS), BF),
            pltpu.VMEM((ROWS, SLOTS, HALF, ORB), BF),
            pltpu.VMEM((ROWS, SLOTS, HALF, ORB), BF),
            pltpu.VMEM(block, F32),
            pltpu.VMEM(block, BF),
            pltpu.VMEM(block, BF),
            pltpu.VMEM(block, F32),
            pltpu.VMEM((2, REACH, HALF, COLS), BF),
            pltpu.VMEM((2, REACH, HALF, COLS), BF),
            pltpu.VMEM(block, BF),
            pltpu.VMEM(block, BF),
            pltpu.VMEM(block, BF),
            pltpu.VMEM((ROWS, 1, ORB), F32),
            pltpu.VMEM((8, ROWS, ORB), F32),
            dma((3,)), dma((2, 2, STEPS)), dma((2, STEPS + 3)),
            dma((2, STEPS)), dma((2, STEPS)),
            dma((2, STEPS)), dma((2, STEPS)),
            dma((2, 3)), dma((2, 3)),
            dma((7,)), dma((7,)),
        ],
        compiler_params=pltpu.CompilerParams(
            collective_id=0, has_side_effects=True, vmem_limit_bytes=62_000_000
        ),
        name="chebyshev",
    )(block_mask, atom_owner, term_now, term_prev, cotangent, ham_blocks, ham_slope)


def solution(mesh):
    return jax.shard_map(
        local,
        mesh=mesh,
        in_specs=(
            P("rows", "layers", "cols"),
            P("rows", "layers", "cols"),
            P("rows", None, "cols"),
            P("rows", None, "layers", None),
            P("rows", None),
            P("rows", None, "layers", None),
            P("rows", None),
        ),
        out_specs=(P("rows", "layers", "cols"), P("rows", "layers", "cols"), P("rows", None)),
        check_vma=False,
    )
```

time: 439 us -> 63.1 us (0.14)
  matrix products: 358 us -> 0 us
  Pallas kernels: 0 us -> 56.9 us
  local copies, waits for them, and re-layouts: 30.7 us -> 4.57 us
  starting transfers between devices: 16.5 us -> 0 us
  other arithmetic: 13.7 us -> 0 us
  between operations: 14.1 us -> 0.65 us
    dot_general x76 -> x0, matrix products: 358 us -> none  [the longest x25 180 us: apply_advance(): jnp.einsum('bnm,bnc->bmc', masked, window, preferred_element_type=jnp.flo...]
    pallas_call x0 -> x1, Pallas kernels: none -> 56.9 us  [local(): pl.pallas_call(kernel, out_shape=(jax.ShapeDtypeStruct(block, BF), jax.Sh...]
    ppermute x4 -> x0, starting transfers between devices: 11.9 us -> none  [the longest x2 5.35 us: from_behind(): return lax.ppermute(value, axis, pairs)]
    unnamed x14 -> x7, local copies, waits for them, and re-layouts: 16.4 us -> 4.57 us
    slice x3 -> x0, local copies, waits for them, and re-layouts: 9.1 us -> none  [the longest x1 4.01 us: local(): from_above = from_behind(pushed[:reach_rows], 'rows', -1)]
    convert_element_type x52 -> x0, other arithmetic: 6.06 us -> none  [the longest x1 4.07 us: local(): (2.0 * forward - term_prev.astype(jnp.float32)).astype(jnp.bfloat16)]
    all_to_all x1 -> x0, starting transfers between devices: 4.48 us -> none  [copy_for_each(): return lax.all_to_all(copies, axis, split_axis=0, concat_axis=0, tiled=True)]
  transfers between devices with their start and end apart: 6 -> 0, of which waited for: 1 -> 0; matrix products, arithmetic and copies ran while one was open for 90% -> 0% of each run, Pallas kernels for 0% -> 0%
where the time goes in v1:
time: 63.1 us; the launch traced here: 62.1 us
  Pallas kernels  56.9 us (90%)
  local copies, waits for them, and re-layouts  4.57 us (7%)
  between operations  0.65 us (1%)
    pallas_call x1, Pallas kernels, local(): pl.pallas_call(kernel, out_shape=(jax.ShapeDtypeStruct(block, BF), jax.Sh...  56.9 us
    unnamed x7, local copies, waits for them, and re-layouts  4.57 us

profile of v1, /device:TPU:0, one launch (start us, length us, event | category | flops | bytes accessed | tf_op | source)
XLA Modules:
  0.0 62.1 jit_solution(2521485993310597285)
XLA Ops:
  0.6 56.9 %chebyshev.1 = (bf16[24,64,512]{2,1,0:T(8,128)(2,1)}, bf16[24,64,512]{2,1,0:T(8,128)(2,1)}, f32[24,64]{1,0:T(8,128)}) custom-call(s32[24,25]{1,0:T(8,128)} %mask.1, s32[24,128]{1,0:T(8,128)} %owner.1, bf16[24,64,512]{2,1,0:T(8,128)(2,1)} %tn.1, bf16[24,64,512]{2,1,0:T(8,128)(2,1)} %tp.1, bf16[24,128,512]{2,1,0:T(8,128)(2,1)} %cot_h.1, ...), custom_call_target="tpu_custom_call" | custom-call | tf_op jit(solution)/shard_map/chebyshev/pallas_call | solution.py:291
  57.5 0.0 copy-start
  57.5 2.8 %copy.13 = bf16[24,64,512]{2,1,0:T(8,128)(2,1)} copy(bf16[24,64,512]{2,1,0:T(8,128)(2,1)} %get-tuple-element.6) | data formatting | bytes 3145728
  60.3 0.0 copy-done
  60.3 0.0 copy-start.1
  60.3 1.1 %copy.14 = bf16[24,64,512]{2,1,0:T(8,128)(2,1)} copy(bf16[24,64,512]{2,1,0:T(8,128)(2,1)S(1)} %copy-done) | data formatting | bytes 3145728
  61.5 0.0 copy-done.1
  61.5 0.6 copy.15
Async XLA Ops:
  57.5 2.8 %copy-start = (bf16[24,64,512]{2,1,0:T(8,128)(2,1)S(1)}, bf16[24,64,512]{2,1,0:T(8,128)(2,1)}, u32[]{:S(2)}) copy-start(bf16[24,64,512]{2,1,0:T(8,128)(2,1)} %get-tuple-element.7) | copy-start | bytes 4718596
  60.3 1.1 %copy-start.1 = (f32[24,64]{1,0:T(8,128)S(1)}, f32[24,64]{1,0:T(8,128)}, u32[]{:S(2)}) copy-start(f32[24,64]{1,0:T(8,128)} %get-tuple-element.8) | copy-start | bytes 18436

commit v2 on v1

v2 whole, which is shorter than its diff:
```python
import jax
import jax.numpy as jnp
from jax import lax
from jax.experimental import pallas as pl
from jax.experimental.pallas import tpu as pltpu
from jax.sharding import PartitionSpec as P

BF = jnp.bfloat16
F32 = jnp.float32
MESH = pl.DeviceIdType.MESH

ROWS = 24
HALF = 64
ORB = 128
COLS = 512
SLOTS = 25
REACH = 12
STEPS = 6


def remote(src, dst, send_sem, recv_sem, device):
    return pltpu.make_async_remote_copy(
        src_ref=src, dst_ref=dst, send_sem=send_sem, recv_sem=recv_sem,
        device_id=device, device_id_type=MESH,
    )


def kernel(
    mask_h, owner_h, tn, tp, cot_h, ham_h, slope_h,
    tno, gro, fo,
    mask, owner, ext, tt, cot, ham, slope, own, xs, xr, bown, bs, br, prev, rf, fbuf,
    lsem, csem, hsem, hs, hr, xss, xrs, bss, bsr, fs, fr,
):
    row = lax.axis_index("rows")
    col = lax.axis_index("cols")
    lay = lax.axis_index("layers")
    up = {"rows": lax.rem(row + 1, 16)}
    down = {"rows": lax.rem(row + 15, 16)}
    partner = {"layers": 1 - lay}
    me = col * 2 + lay

    def ring(index):
        return {"cols": index // 2, "layers": index % 2}

    def load_term():
        return pltpu.make_async_copy(tn, ext.at[pl.ds(REACH, ROWS)], lsem.at[0])

    def load_mask():
        return pltpu.make_async_copy(mask_h, mask, lsem.at[2])

    def load_owner():
        return pltpu.make_async_copy(owner_h, owner, lsem.at[3])

    load_term().start()
    barrier = pltpu.get_barrier_semaphore()
    pl.semaphore_signal(barrier, 1, device_id=up, device_id_type=MESH)
    pl.semaphore_signal(barrier, 1, device_id=down, device_id_type=MESH)
    for o in range(1, 8):
        pl.semaphore_signal(
            barrier, 1, device_id=ring(lax.rem(me + o, 8)), device_id_type=MESH
        )

    def load_cot(part):
        at = (pl.ds(10, 4), pl.ds(0, 10), pl.ds(14, 10))[part]
        return pltpu.make_async_copy(cot_h.at[at], cot.at[at], csem.at[part])

    def load_prev():
        return pltpu.make_async_copy(tp, prev, lsem.at[1])

    def load_blocks(k):
        copies = []
        for side, first in ((0, 10 - 2 * k), (1, 12 + 2 * k)):
            at = pl.ds(first, 2)
            copies.append(pltpu.make_async_copy(ham_h.at[at], ham.at[at], hsem.at[0, side, k]))
            copies.append(
                pltpu.make_async_copy(slope_h.at[at], slope.at[at], hsem.at[1, side, k])
            )
        return copies

    load_mask().start()
    for c in load_blocks(0):
        c.start()
    load_cot(0).start()

    def rows_of(s, lone):
        return (1 - s, 1) if lone else (2 - 2 * s, 2)

    def to_up(s, lone):
        back, n = rows_of(s, lone)
        return remote(
            tn.at[pl.ds(22 + back, n)] if lone else ext.at[pl.ds(34 + back, n)], ext.at[pl.ds(10 + back, n)],
            hs.at[0, s], hr.at[0, s], up,
        )

    def to_down(s, lone):
        n = 1 if lone else 2
        on = s if lone else 2 * s - 2
        return remote(
            tn.at[pl.ds(on, n)] if lone else ext.at[pl.ds(12 + on, n)], ext.at[pl.ds(36 + on, n)],
            hs.at[1, s], hr.at[1, s], down,
        )

    with jax.named_scope("rg_barrier"):
        pl.semaphore_wait(barrier, 9)
    for s in range(2):
        to_up(s, True).start()
        to_down(s, True).start()
    with jax.named_scope("rg_term"):
        load_term().wait()
    for s in range(2, STEPS + 1):
        to_up(s, False).start()
        to_down(s, False).start()
    load_cot(1).start()
    load_cot(2).start()
    for k in range(1, STEPS):
        for c in load_blocks(k):
            c.start()
    load_prev().start()
    load_owner().start()

    def turn(pair):
        tt[pair] = ext[pl.ds(2 * pair, 2)].reshape(ORB, COLS).T

    def turn_local(p, carry):
        turn(p + 6)
        return carry

    lax.fori_loop(0, 12, turn_local, 0)

    def mask_rows(k, carry):
        for c in load_blocks(k):
            c.wait()
        for first in (10 - 2 * k, 12 + 2 * k):
            for r in range(2):
                i = first + r
                for d in range(SLOTS):
                    kept = jnp.full((HALF, ORB), mask[i, d].astype(F32), F32).astype(BF)
                    ham[i, d] = ham[i, d] * kept
                    slope[i, d] = slope[i, d] * kept
        return carry

    def send_partial(s, side, lone):
        n = 1 if lone else 2
        first = (11 - s if lone else 12 - 2 * s) if side == 0 else (12 + s if lone else 10 + 2 * s)
        at = pl.ds(first, n)
        return remote(
            xs.at[at], xr.at[at], xss.at[side, s], xrs.at[side, s], partner
        )

    edge = jnp.zeros((HALF, 2 * ORB), BF)

    def stacked(i, before, after):
        w = jnp.concatenate(
            [ham[i].reshape(SLOTS * HALF, ORB), slope[i].reshape(SLOTS * HALF, ORB)],
            axis=1,
        )
        parts = [w]
        if before:
            parts = [jnp.zeros((HALF * before, 2 * ORB), BF)] + parts
        if after:
            parts = parts + [jnp.zeros((HALF * after, 2 * ORB), BF)]
        return jnp.concatenate(parts, axis=0)

    def product(pair, pairs, rows):
        lhs = jnp.concatenate([tt[pair + g] for g in range(pairs)], axis=1)
        weights = [stacked(i, r, 2 * pairs - SLOTS - r) for i, r in rows]
        out = jnp.dot(lhs, jnp.concatenate(weights, axis=1), preferred_element_type=F32)
        for n, (i, _) in enumerate(rows):
            f = out[:, 2 * n * ORB : (2 * n + 1) * ORB].T
            low, high = f[:HALF], f[HALF:]
            own[i] = jnp.where(lay == 0, low, high)
            xs[i] = jnp.where(lay == 0, high, low).astype(BF)
            g = out[:, (2 * n + 1) * ORB : (2 * n + 2) * ORB]
            turned = cot[i].T.astype(F32)
            rf[i] = 2.0 * jnp.sum(turned * g, axis=0, keepdims=True)

    def forward(s, carry):
        to_up(s, False).wait_recv()
        to_down(s, False).wait_recv()
        turn(6 - s)
        turn(17 + s)
        for side in range(2):
            pair = 6 - s if side == 0 else 5 + s
            product(pair, 13, ((2 * pair, 0), (2 * pair + 1, 1)))

            @pl.when(s < STEPS)
            def _():
                send_partial(s, side, False).start()

        return carry

    def push_group(g):
        i0, i1 = max(0, 4 * g - 24), min(ROWS - 1, 4 * g + 3)
        parts = []
        for i in range(i0, i1 + 1):
            d0 = 4 * g - i
            lo, hi = max(0, -d0), min(4, SLOTS - d0)
            p = []
            if lo:
                p.append(jnp.zeros((HALF * lo, ORB), BF))
            p.append(ham[i, d0 + lo : d0 + hi].reshape((hi - lo) * HALF, ORB))
            if hi < 4:
                p.append(jnp.zeros((HALF * (4 - hi), ORB), BF))
            parts.append(jnp.concatenate(p, axis=0) if len(p) > 1 else p[0])
        out = jnp.dot(
            jnp.concatenate(parts, axis=1),
            cot[i0 : i1 + 1].reshape((i1 - i0 + 1) * ORB, COLS),
            preferred_element_type=F32,
        )
        return out.reshape(4, HALF, COLS)

    def send_pushed(side, g):
        at = pl.ds(4 * g, 4)
        return remote(
            bs.at[side, at], br.at[1 - side, at], bss.at[side, g], bsr.at[side, g],
            down if side == 0 else up,
        )

    with jax.named_scope("rg_mask0"):
        load_mask().wait()
        mask_rows(0, 0)
    load_cot(0).wait()
    nothing = jnp.zeros((HALF, COLS), BF)
    with jax.named_scope("rg_halo0"):
        to_up(0, True).wait_recv()
        to_down(0, True).wait_recv()
    with jax.named_scope("rg_fwd0"):
        tt[5] = jnp.concatenate([nothing, ext[11]], axis=0).T
        tt[18] = jnp.concatenate([ext[36], nothing], axis=0).T
        product(5, 14, ((11, 1), (12, 2)))
        for side in range(2):
            send_partial(0, side, True).start()
    with jax.named_scope("rg_halo1"):
        to_up(1, True).wait_recv()
        to_down(1, True).wait_recv()
    with jax.named_scope("rg_fwd1"):
        turn(5)
        turn(18)
        product(5, 14, ((10, 0), (13, 3)))
        for side in range(2):
            send_partial(1, side, True).start()
    with jax.named_scope("rg_mask1"):
        load_cot(1).wait()
        load_cot(2).wait()
        lax.fori_loop(1, STEPS, mask_rows, 0)
    with jax.named_scope("rg_fwd2"):
        forward(2, 0)
    with jax.named_scope("rg_edges"):
        for g in range(3):
            bs[0, 4 * g : 4 * g + 4] = push_group(g).astype(BF)
            bs[1, 4 * g : 4 * g + 4] = push_group(9 + g).astype(BF)
            send_pushed(0, g).start()
            send_pushed(1, g).start()
    with jax.named_scope("rg_fwd"):
        lax.fori_loop(3, STEPS + 1, forward, 0)
    load_owner().wait()

    atoms = lax.broadcasted_iota(jnp.int32, (HALF, ORB), 0)
    lanes = lax.broadcasted_iota(jnp.int32, (HALF, ORB), 1)

    def gather_atoms(i, total):
        mine = jnp.where(owner[pl.ds(i, 1)] == atoms, rf[i], 0.0)
        summed = jnp.sum(mine, axis=1, keepdims=True)
        return total + jnp.where(lanes == i, summed, 0.0)

    total = lax.fori_loop(0, ROWS, gather_atoms, jnp.zeros((HALF, ORB), F32))
    total = jnp.concatenate([total, jnp.zeros((HALF, ORB), F32)], axis=0).T
    fbuf[me] = total[:ROWS]

    def send_force(o):
        return remote(
            fbuf.at[me], fbuf.at[me], fs.at[o - 1], fr.at[o - 1],
            ring(lax.rem(me + o, 8)),
        )

    def take_force(o):
        slot = lax.rem(me + 8 - o, 8)
        return remote(
            fbuf.at[slot], fbuf.at[slot], fs.at[o - 1], fr.at[o - 1],
            ring(lax.rem(me + o, 8)),
        )

    for o in range(1, 8):
        send_force(o).start()
    for side in range(2):
        send_partial(STEPS, side, False).start()

    with jax.named_scope("rg_push"):
        for g in range(3, 9):
            bown[4 * (g - 3) : 4 * (g - 2)] = push_group(g)

    load_prev().wait()

    def finish_term(s, lone):
        for side in range(2):
            n = 1 if lone else 2
            first = (11 - s if lone else 12 - 2 * s) if side == 0 else (12 + s if lone else 10 + 2 * s)
            at = pl.ds(first, n)
            with jax.named_scope("rg_xW"):
                send_partial(s, side, lone).wait_recv()
            both = own[at] + xr[at].astype(F32)
            tno[at] = (2.0 * both - prev[at].astype(F32)).astype(BF)

    def finish_grad(g):
        for side in range(2):
            at = pl.ds(12 * side + 4 * g, 4)
            with jax.named_scope("rg_bW"):
                send_pushed(1 - side, g).wait_recv()
            both = bown[at] + br[side, pl.ds(4 * g, 4)].astype(F32)
            gro[at] = (2.0 * both).astype(BF)

    def finish_loop(s, carry):
        finish_term(s, False)
        return carry

    finish_term(0, True)
    finish_term(1, True)
    finish_grad(0)
    lax.fori_loop(2, STEPS - 1, finish_loop, 0)
    finish_grad(1)
    finish_term(STEPS - 1, False)
    finish_grad(2)
    with jax.named_scope("rg_forceW"):
        for o in range(1, 8):
            take_force(o).wait_recv()
    summed = fbuf[0]
    for s in range(1, 8):
        summed = summed + fbuf[s]
    fo[...] = summed[:, :HALF]
    with jax.named_scope("rg_last"):
        finish_term(STEPS, False)

    with jax.named_scope("rg_tail"):
        for s in range(STEPS + 1):
            to_up(s, s < 2).wait_send()
            to_down(s, s < 2).wait_send()
            for side in range(2):
                send_partial(s, side, s < 2).wait_send()
        for g in range(3):
            for side in range(2):
                send_pushed(side, g).wait_send()
        for o in range(1, 8):
            send_force(o).wait_send()


def write_out(a, b, c, ao, bo, co, sem):
    copies = [
        pltpu.make_async_copy(x, y, sem.at[n])
        for n, (x, y) in enumerate(((a, ao), (b, bo), (c, co)))
    ]
    for copy in copies:
        copy.start()
    for copy in copies:
        copy.wait()


def local(term_now, term_prev, cotangent, ham_blocks, block_mask, ham_slope, atom_owner):
    anyspace = pl.BlockSpec(memory_space=pl.ANY)
    dma = pltpu.SemaphoreType.DMA
    block = (ROWS, HALF, COLS)
    vmem = pl.BlockSpec(memory_space=pltpu.VMEM)
    shapes = ((block, BF), (block, BF), ((ROWS, HALF), F32))
    results = pl.pallas_call(
        kernel,
        out_shape=tuple(pltpu.VMEM(*s) for s in shapes),
        in_specs=[anyspace] * 7,
        out_specs=(vmem, vmem, vmem),
        scratch_shapes=[
            pltpu.SMEM((ROWS, SLOTS), jnp.int32),
            pltpu.VMEM((ROWS, ORB), jnp.int32),
            pltpu.VMEM((ROWS + 2 * REACH, HALF, COLS), BF),
            pltpu.VMEM((24, COLS, ORB), BF),
            pltpu.VMEM((ROWS, ORB, COLS), BF),
            pltpu.VMEM((ROWS, SLOTS, HALF, ORB), BF),
            pltpu.VMEM((ROWS, SLOTS, HALF, ORB), BF),
            pltpu.VMEM(block, F32),
            pltpu.VMEM(block, BF),
            pltpu.VMEM(block, BF),
            pltpu.VMEM(block, F32),
            pltpu.VMEM((2, REACH, HALF, COLS), BF),
            pltpu.VMEM((2, REACH, HALF, COLS), BF),
            pltpu.VMEM(block, BF),
            pltpu.VMEM((ROWS, 1, ORB), F32),
            pltpu.VMEM((8, ROWS, ORB), F32),
            dma((4,)), dma((3,)), dma((2, 2, STEPS)),
            dma((2, STEPS + 1)), dma((2, STEPS + 1)),
            dma((2, STEPS + 1)), dma((2, STEPS + 1)),
            dma((2, 3)), dma((2, 3)),
            dma((7,)), dma((7,)),
        ],
        compiler_params=pltpu.CompilerParams(
            collective_id=0, has_side_effects=True, vmem_limit_bytes=54_000_000
        ),
        name="chebyshev",
    )(block_mask, atom_owner, term_now, term_prev, cotangent, ham_blocks, ham_slope)
    return pl.pallas_call(
        write_out,
        out_shape=tuple(jax.ShapeDtypeStruct(*s) for s in shapes),
        in_specs=[vmem] * 3,
        out_specs=(anyspace,) * 3,
        scratch_shapes=[dma((3,))],
        compiler_params=pltpu.CompilerParams(vmem_limit_bytes=4_000_000),
        name="write_out",
    )(*results)


def solution(mesh):
    return jax.shard_map(
        local,
        mesh=mesh,
        in_specs=(
            P("rows", "layers", "cols"),
            P("rows", "layers", "cols"),
            P("rows", None, "cols"),
            P("rows", None, "layers", None),
            P("rows", None),
            P("rows", None, "layers", None),
            P("rows", None),
        ),
        out_specs=(P("rows", "layers", "cols"), P("rows", "layers", "cols"), P("rows", None)),
        check_vma=False,
    )
```

time: 63.1 us -> 53.7 us (0.85); the launches traced: 62.1 us -> 53.5 us
  local copies, waits for them, and re-layouts: 4.57 us -> 0 us
  Pallas kernels: 56.9 us -> 52.9 us
    unnamed x7 -> x0, local copies, waits for them, and re-layouts: 4.57 us -> none
    pallas_call x1 -> x2, Pallas kernels: 56.9 us -> 52.9 us  [the longest x1 51.2 us: local(): pl.pallas_call(kernel, out_shape=tuple((pltpu.VMEM(*s) for s in shapes)),...]
where the time goes in v2:
time: 53.7 us; the launch traced here: 53.5 us
  Pallas kernels  52.9 us (99%)
  between operations  0.64 us (1%)
    pallas_call x1, Pallas kernels, local(): pl.pallas_call(kernel, out_shape=tuple((pltpu.VMEM(*s) for s in shapes)),...  51.2 us
    pallas_call x1, Pallas kernels, local(): pl.pallas_call(write_out, out_shape=tuple((jax.ShapeDtypeStruct(*s) for s...  1.69 us

profile of v2, /device:TPU:0, one launch (start us, length us, event | category | flops | bytes accessed | tf_op | source)
XLA Modules:
  0.0 53.5 jit_solution(15119959352855625714)
XLA Ops:
  0.6 51.2 %chebyshev.1 = (bf16[24,64,512]{2,1,0:T(8,128)(2,1)S(1)}, bf16[24,64,512]{2,1,0:T(8,128)(2,1)S(1)}, f32[24,64]{1,0:T(8,128)S(1)}) custom-call(s32[24,25]{1,0:T(8,128)} %mask_h.1, s32[24,128]{1,0:T(8,128)} %owner_h.1, bf16[24,64,512]{2,1,0:T(8,128)(2,1)} %tn.1, bf16[24,64,512]{2,1,0:T(8,128)(2,1)} %tp.1, bf16[24,128,512]{2,1,0:T(8,128)(2,1)} %cot_h.1, ...), custom_call_target="tpu_custom_call" | custom-call | tf_op jit(solution)/shard_map/chebyshev/pallas_call | solution.py:363
  51.8 1.7 %write_out.1 = (bf16[24,64,512]{2,1,0:T(8,128)(2,1)}, bf16[24,64,512]{2,1,0:T(8,128)(2,1)}, f32[24,64]{1,0:T(8,128)}) custom-call(bf16[24,64,512]{2,1,0:T(8,128)(2,1)S(1)} %get-tuple-element.6.a, bf16[24,64,512]{2,1,0:T(8,128)(2,1)S(1)} %get-tuple-element.7.b, f32[24,64]{1,0:T(8,128)S(1)} %get-tuple-element.8.c), custom_call_target="tpu_custom_call" | custom-call | tf_op jit(solution)/shard_map/write_out/pallas_call | solution.py:396

commit v3 on v2

v3 whole, which is shorter than its diff:
```python
import jax
import jax.numpy as jnp
from jax import lax
from jax.experimental import pallas as pl
from jax.experimental.pallas import tpu as pltpu
from jax.sharding import PartitionSpec as P

BF = jnp.bfloat16
F32 = jnp.float32
MESH = pl.DeviceIdType.MESH

ROWS = 24
HALF = 64
ORB = 128
COLS = 512
SLOTS = 25
REACH = 12
STEPS = 6
LONE = ((0, 0, 128), (0, 128, 128), (0, 256, 256), (1, 0, 256), (1, 256, 256))
FIRST = len(LONE)
LAST = FIRST + STEPS - 2


def remote(src, dst, send_sem, recv_sem, device):
    return pltpu.make_async_remote_copy(
        src_ref=src, dst_ref=dst, send_sem=send_sem, recv_sem=recv_sem,
        device_id=device, device_id_type=MESH,
    )


def kernel(
    mask_h, owner_h, tn, tp, cot_h, ham_h, slope_h,
    tno, gro, fo,
    mask, owner, ext, tt, cot, ham, slope, own, xs, xr, bown, bs, br, prev, to, go, rf, fbuf, fsum,
    lsem, hsem, osem, hs, hr, xss, xrs, bss, bsr, fs, fr,
):
    row = lax.axis_index("rows")
    col = lax.axis_index("cols")
    lay = lax.axis_index("layers")
    up = {"rows": lax.rem(row + 1, 16)}
    down = {"rows": lax.rem(row + 15, 16)}
    partner = {"layers": 1 - lay}
    me = col * 2 + lay

    def ring(index):
        return {"cols": index // 2, "layers": index % 2}

    def load_term():
        return pltpu.make_async_copy(tn, ext.at[pl.ds(REACH, ROWS)], lsem.at[0])

    def load_mask():
        return pltpu.make_async_copy(mask_h, mask, lsem.at[2])

    def load_owner():
        return pltpu.make_async_copy(owner_h, owner, lsem.at[3])

    load_term().start()
    barrier = pltpu.get_barrier_semaphore()
    pl.semaphore_signal(barrier, 1, device_id=up, device_id_type=MESH)
    pl.semaphore_signal(barrier, 1, device_id=down, device_id_type=MESH)
    for o in range(1, 8):
        pl.semaphore_signal(
            barrier, 1, device_id=ring(lax.rem(me + o, 8)), device_id_type=MESH
        )

    def load_cot(part):
        at = (pl.ds(10, 4), pl.ds(0, 10), pl.ds(14, 10))[part]
        return pltpu.make_async_copy(cot_h.at[at], cot.at[at], lsem.at[4 if part else 5])

    def cot_rest():
        return pltpu.make_async_copy(
            cot_h.at[pl.ds(0, 20)], cot.at[pl.ds(0, 20)], lsem.at[4]
        )

    def load_prev():
        return pltpu.make_async_copy(tp, prev, lsem.at[1])

    def load_blocks(k):
        copies = []
        for first in (10 - 2 * k, 12 + 2 * k):
            at = pl.ds(first, 2)
            copies.append(pltpu.make_async_copy(ham_h.at[at], ham.at[at], hsem.at[k]))
            copies.append(pltpu.make_async_copy(slope_h.at[at], slope.at[at], hsem.at[k]))
        return copies

    def have_blocks(k):
        at = pl.ds(0, 8)
        pltpu.make_async_copy(ham_h.at[at], ham.at[at], hsem.at[k]).wait()

    load_mask().start()
    for c in load_blocks(0):
        c.start()
    load_cot(0).start()

    def to_up(s):
        return remote(
            ext.at[pl.ds(42 - 2 * s, 2)], ext.at[pl.ds(18 - 2 * s, 2)],
            hs.at[0], hr.at[s], up,
        )

    def to_down(s):
        return remote(
            ext.at[pl.ds(4 + 2 * s, 2)], ext.at[pl.ds(28 + 2 * s, 2)],
            hs.at[0], hr.at[s], down,
        )

    def lone_up(u):
        away, c0, n = LONE[u]
        cs = pl.ds(c0, n)
        return remote(
            ext.at[pl.ds(35 - away, 1), :, cs], ext.at[pl.ds(11 - away, 1), :, cs],
            hs.at[0], hr.at[u], up,
        )

    def lone_down(u):
        away, c0, n = LONE[u]
        cs = pl.ds(c0, n)
        return remote(
            ext.at[pl.ds(12 + away, 1), :, cs], ext.at[pl.ds(36 + away, 1), :, cs],
            hs.at[0], hr.at[u], down,
        )

    def halo_bytes(rows, cs, sem):
        at = pl.ds(REACH, rows), slice(None), cs
        return remote(ext.at[at], ext.at[at], hs.at[0], sem, up)

    def have_lone(u):
        halo_bytes(2, pl.ds(LONE[u][1], LONE[u][2]), hr.at[u]).wait_recv()

    def have_halo(s):
        halo_bytes(4, pl.ds(0, COLS), hr.at[s]).wait_recv()

    def start_lone(u):
        lone_up(u).start()
        lone_down(u).start()

    def start_halo(s):
        to_up(s).start()
        to_down(s).start()

    with jax.named_scope("rg_term"):
        load_term().wait()
    with jax.named_scope("rg_barrier"):
        pl.semaphore_wait(barrier, 9)
    for u in range(3):
        start_lone(u)

    def turn(pair):
        tt[pair] = ext[pl.ds(2 * pair, 2)].reshape(ORB, COLS).T

    def turn_local(p, carry):
        turn(p + 6)
        return carry

    lax.fori_loop(0, 6, turn_local, 0)
    start_lone(3)
    for c in load_blocks(1):
        c.start()
    lax.fori_loop(6, 12, turn_local, 0)
    start_lone(4)
    load_cot(1).start()
    load_cot(2).start()

    def mask_rows(k, carry):
        have_blocks(k)
        for first in (10 - 2 * k, 12 + 2 * k):
            for r in range(2):
                i = first + r
                for d in range(SLOTS):
                    kept = jnp.full((HALF, ORB), mask[i, d].astype(F32), F32).astype(BF)
                    ham[i, d] = ham[i, d] * kept
                    slope[i, d] = slope[i, d] * kept
        return carry

    def step_rows(s, side):
        return 18 - 2 * s if side == 0 else 4 + 2 * s

    def send_partial(s, side):
        at = pl.ds(step_rows(s, side), 2)
        return remote(
            xs.at[at], xr.at[at], xss.at[0], xrs.at[s], partner
        )

    def lone_at(u, side):
        away, c0, n = LONE[u]
        return pl.ds(12 + away if side else 11 - away, 1), slice(None), pl.ds(c0, n)

    def send_lone(u, side):
        at = lone_at(u, side)
        return remote(
            xs.at[at], xr.at[at], xss.at[0], xrs.at[u], partner
        )

    def stacked(i, before, after):
        w = jnp.concatenate(
            [ham[i].reshape(SLOTS * HALF, ORB), slope[i].reshape(SLOTS * HALF, ORB)],
            axis=1,
        )
        parts = [w]
        if before:
            parts = [jnp.zeros((HALF * before, 2 * ORB), BF)] + parts
        if after:
            parts = parts + [jnp.zeros((HALF * after, 2 * ORB), BF)]
        return jnp.concatenate(parts, axis=0)

    def product(pair, pairs, rows, c0=0, cols=COLS):
        cs = slice(c0, c0 + cols)
        lhs = jnp.concatenate([tt[pair + g, cs] for g in range(pairs)], axis=1)
        weights = [stacked(i, r, 2 * pairs - SLOTS - r) for i, r in rows]
        out = jnp.dot(lhs, jnp.concatenate(weights, axis=1), preferred_element_type=F32)
        for n, (i, _) in enumerate(rows):
            f = out[:, 2 * n * ORB : (2 * n + 1) * ORB].T
            low, high = f[:HALF], f[HALF:]
            own[i, :, cs] = jnp.where(lay == 0, low, high)
            xs[i, :, cs] = jnp.where(lay == 0, high, low).astype(BF)
            g = out[:, (2 * n + 1) * ORB : (2 * n + 2) * ORB]
            turned = cot[i, :, cs].T.astype(F32)
            part = 2.0 * jnp.sum(turned * g, axis=0, keepdims=True)
            rf[i] = rf[i] + part if c0 else part

    nothing = jnp.zeros((HALF, COLS), BF)

    def forward_lone(u):
        away, c0, n = LONE[u]
        cs = slice(c0, c0 + n)
        with jax.named_scope("rg_halo"):
            have_lone(u)
        low = jnp.concatenate([ext[10, :, cs] if away else nothing[:, :n], ext[11, :, cs]], axis=0)
        high = jnp.concatenate([ext[36, :, cs], ext[37, :, cs] if away else nothing[:, :n]], axis=0)
        tt[5, cs] = low.T
        tt[18, cs] = high.T
        product(5, 14, ((10, 0), (13, 3)) if away else ((11, 1), (12, 2)), c0, n)
        for side in range(2):
            send_lone(u, side).start()

    def forward(s, carry):
        with jax.named_scope("rg_halo"):
            have_halo(s)
        turn(9 - s)
        turn(14 + s)
        for side in range(2):
            pair = 9 - s if side == 0 else 2 + s
            product(pair, 13, ((2 * pair, 0), (2 * pair + 1, 1)))

            @pl.when(s < LAST)
            def _():
                send_partial(s, side).start()

        return carry

    def push_group(g):
        i0, i1 = max(0, 4 * g - 24), min(ROWS - 1, 4 * g + 3)
        parts = []
        for i in range(i0, i1 + 1):
            d0 = 4 * g - i
            lo, hi = max(0, -d0), min(4, SLOTS - d0)
            p = []
            if lo:
                p.append(jnp.zeros((HALF * lo, ORB), BF))
            p.append(ham[i, d0 + lo : d0 + hi].reshape((hi - lo) * HALF, ORB))
            if hi < 4:
                p.append(jnp.zeros((HALF * (4 - hi), ORB), BF))
            parts.append(jnp.concatenate(p, axis=0) if len(p) > 1 else p[0])
        out = jnp.dot(
            jnp.concatenate(parts, axis=1),
            cot[i0 : i1 + 1].reshape((i1 - i0 + 1) * ORB, COLS),
            preferred_element_type=F32,
        )
        return out.reshape(4, HALF, COLS)

    def send_pushed(side, g):
        at = pl.ds(4 * g, 4)
        return remote(
            bs.at[side, at], br.at[1 - side, at], bss.at[0], bsr.at[g],
            down if side == 0 else up,
        )

    with jax.named_scope("rg_mask0"):
        load_mask().wait()
        mask_rows(0, 0)
    load_cot(0).wait()
    start_halo(5)
    for k in range(2, STEPS):
        for c in load_blocks(k):
            c.start()
    load_prev().start()
    load_owner().start()
    with jax.named_scope("rg_fwd0"):
        for u in range(3):
            forward_lone(u)
    start_halo(6)
    with jax.named_scope("rg_fwd1"):
        for u in range(3, 5):
            forward_lone(u)
    start_halo(7)
    with jax.named_scope("rg_mask1"):
        cot_rest().wait()
        mask_rows(1, 0)
    start_halo(8)
    with jax.named_scope("rg_fwd2"):
        forward(FIRST, 0)
    start_halo(9)
    with jax.named_scope("rg_fwd3"):
        mask_rows(2, 0)
        forward(FIRST + 1, 0)
    with jax.named_scope("rg_mask2"):
        lax.fori_loop(3, STEPS, mask_rows, 0)
    with jax.named_scope("rg_edges"):
        for g in range(3):
            bs[0, 4 * g : 4 * g + 4] = push_group(g).astype(BF)
            bs[1, 4 * g : 4 * g + 4] = push_group(9 + g).astype(BF)
            send_pushed(0, g).start()
            send_pushed(1, g).start()
    with jax.named_scope("rg_fwd"):
        lax.fori_loop(FIRST + 2, LAST + 1, forward, 0)
    load_owner().wait()

    atoms = lax.broadcasted_iota(jnp.int32, (HALF, ORB), 0)
    lanes = lax.broadcasted_iota(jnp.int32, (HALF, ORB), 1)

    def gather_atoms(i, total):
        mine = jnp.where(owner[pl.ds(i, 1)] == atoms, rf[i], 0.0)
        summed = jnp.sum(mine, axis=1, keepdims=True)
        return total + jnp.where(lanes == i, summed, 0.0)

    total = lax.fori_loop(0, ROWS, gather_atoms, jnp.zeros((HALF, ORB), F32))
    total = jnp.concatenate([total, jnp.zeros((HALF, ORB), F32)], axis=0).T
    fbuf[me] = total[:ROWS]

    def send_force(o):
        return remote(
            fbuf.at[me], fbuf.at[me], fs.at[0], fr.at[0],
            ring(lax.rem(me + o, 8)),
        )

    def all_forces():
        at = pl.ds(0, 7)
        return remote(fbuf.at[at], fbuf.at[at], fs.at[0], fr.at[0], partner)

    for o in range(1, 8):
        send_force(o).start()
    for side in range(2):
        send_partial(LAST, side).start()

    with jax.named_scope("rg_push"):
        for g in range(3, 9):
            bown[4 * (g - 3) : 4 * (g - 2)] = push_group(g)

    load_prev().wait()

    def out_term(s, side):
        at = pl.ds(step_rows(s, side), 2)
        return pltpu.make_async_copy(to.at[at], tno.at[at], osem.at[0])

    def out_middle():
        at = pl.ds(10, 4)
        return pltpu.make_async_copy(to.at[at], tno.at[at], osem.at[0])

    def out_grad(side, g):
        at = pl.ds(12 * side + 4 * g, 4)
        return pltpu.make_async_copy(go.at[at], gro.at[at], osem.at[1])

    def finish_at(at):
        both = own[at] + xr[at].astype(F32)
        to[at] = (2.0 * both - prev[at].astype(F32)).astype(BF)

    def have_partial(s, rows, cs):
        at = pl.ds(0, rows), slice(None), cs
        with jax.named_scope("rg_xW"):
            remote(xs.at[at], xr.at[at], xss.at[0], xrs.at[s], partner).wait_recv()

    def finish_term(s, carry):
        have_partial(s, 4, pl.ds(0, COLS))
        for side in range(2):
            finish_at(pl.ds(step_rows(s, side), 2))
            out_term(s, side).start()
        return carry

    def have_pushed(g):
        at = pl.ds(4 * g, 4)
        remote(bs.at[:, at], br.at[:, at], bss.at[0], bsr.at[g], up).wait_recv()

    def finish_grad(g):
        with jax.named_scope("rg_bW"):
            have_pushed(g)
        for side in range(2):
            at = pl.ds(12 * side + 4 * g, 4)
            both = bown[at] + br[side, pl.ds(4 * g, 4)].astype(F32)
            go[at] = (2.0 * both).astype(BF)
            out_grad(side, g).start()

    for u in range(FIRST):
        have_partial(u, 2, pl.ds(LONE[u][1], LONE[u][2]))
    finish_at(pl.ds(10, 4))
    out_middle().start()
    finish_grad(0)
    lax.fori_loop(FIRST, LAST - 1, finish_term, 0)
    finish_grad(1)
    finish_term(LAST - 1, 0)
    finish_grad(2)
    with jax.named_scope("rg_forceW"):
        all_forces().wait_recv()
    summed = fbuf[0]
    for s in range(1, 8):
        summed = summed + fbuf[s]
    fsum[...] = summed[:, :HALF]
    force_out = pltpu.make_async_copy(fsum, fo, osem.at[2])
    force_out.start()

    with jax.named_scope("rg_sent"):
        sent = ext.at[pl.ds(0, ROWS)]
        remote(sent, sent, hs.at[0], hr.at[0], up).wait_send()
        remote(bs, br, bss.at[0], bsr.at[0], up).wait_send()
        all_forces().wait_send()
        force_out.wait()
        pltpu.make_async_copy(go, gro, osem.at[1]).wait()
    with jax.named_scope("rg_last"):
        finish_term(LAST, 0)
    with jax.named_scope("rg_tail"):
        remote(xs, xr, xss.at[0], xrs.at[0], partner).wait_send()
        pltpu.make_async_copy(to, tno, osem.at[0]).wait()


def write_out(a, b, c, ao, bo, co, sem):
    copies = [pltpu.make_async_copy(c, co, sem.at[0])]
    for n, (x, y) in enumerate(((a, ao), (b, bo))):
        for part in range(4):
            at = pl.ds(6 * part, 6)
            copies.append(pltpu.make_async_copy(x.at[at], y.at[at], sem.at[1 + 4 * n + part]))
    for copy in copies:
        copy.start()
    for copy in copies:
        copy.wait()


def local(term_now, term_prev, cotangent, ham_blocks, block_mask, ham_slope, atom_owner):
    anyspace = pl.BlockSpec(memory_space=pl.ANY)
    dma = pltpu.SemaphoreType.DMA
    block = (ROWS, HALF, COLS)
    shapes = ((block, BF), (block, BF), ((ROWS, HALF), F32))
    results = pl.pallas_call(
        kernel,
        out_shape=tuple(pltpu.VMEM(*s) for s in shapes),
        in_specs=[anyspace] * 7,
        out_specs=(anyspace,) * 3,
        scratch_shapes=[
            pltpu.SMEM((ROWS, SLOTS), jnp.int32),
            pltpu.VMEM((ROWS, ORB), jnp.int32),
            pltpu.VMEM((ROWS + 2 * REACH, HALF, COLS), BF),
            pltpu.VMEM((24, COLS, ORB), BF),
            pltpu.VMEM((ROWS, ORB, COLS), BF),
            pltpu.VMEM((ROWS, SLOTS, HALF, ORB), BF),
            pltpu.VMEM((ROWS, SLOTS, HALF, ORB), BF),
            pltpu.VMEM(block, F32),
            pltpu.VMEM(block, BF),
            pltpu.VMEM(block, BF),
            pltpu.VMEM(block, F32),
            pltpu.VMEM((2, REACH, HALF, COLS), BF),
            pltpu.VMEM((2, REACH, HALF, COLS), BF),
            pltpu.VMEM(block, BF),
            pltpu.VMEM(block, BF),
            pltpu.VMEM(block, BF),
            pltpu.VMEM((ROWS, 1, ORB), F32),
            pltpu.VMEM((8, ROWS, ORB), F32),
            pltpu.VMEM((ROWS, HALF), F32),
            dma((6,)), dma((STEPS,)), dma((3,)),
            dma((1,)), dma((LAST + 1,)),
            dma((1,)), dma((LAST + 1,)),
            dma((1,)), dma((3,)),
            dma((1,)), dma((1,)),
        ],
        compiler_params=pltpu.CompilerParams(
            collective_id=0, has_side_effects=True, vmem_limit_bytes=54_000_000
        ),
        name="chebyshev",
    )(block_mask, atom_owner, term_now, term_prev, cotangent, ham_blocks, ham_slope)
    return pl.pallas_call(
        write_out,
        out_shape=tuple(jax.ShapeDtypeStruct(*s) for s in shapes),
        in_specs=[anyspace] * 3,
        out_specs=(anyspace,) * 3,
        scratch_shapes=[dma((9,))],
        compiler_params=pltpu.CompilerParams(vmem_limit_bytes=4_000_000),
        name="write_out",
    )(*results)


def solution(mesh):
    return jax.shard_map(
        local,
        mesh=mesh,
        in_specs=(
            P("rows", "layers", "cols"),
            P("rows", "layers", "cols"),
            P("rows", None, "cols"),
            P("rows", None, "layers", None),
            P("rows", None),
            P("rows", None, "layers", None),
            P("rows", None),
        ),
        out_specs=(P("rows", "layers", "cols"), P("rows", "layers", "cols"), P("rows", None)),
        check_vma=False,
    )
```

time: 53.7 us -> 52.3 us (0.974)
  Pallas kernels: 52.9 us -> 51.4 us
    pallas_call x1, Pallas kernels: 51.2 us -> 49.6 us  [local(): pl.pallas_call(kernel, out_shape=tuple((pltpu.VMEM(*s) for s in shapes)),...]
where the time goes in v3:
time: 52.3 us; the launch traced here: 52.2 us
  Pallas kernels  51.4 us (98%)
  between operations  0.8 us (2%)
    pallas_call x1, Pallas kernels, local(): pl.pallas_call(kernel, out_shape=tuple((pltpu.VMEM(*s) for s in shapes)),...  49.6 us
    pallas_call x1, Pallas kernels, local(): pl.pallas_call(write_out, out_shape=tuple((jax.ShapeDtypeStruct(*s) for s...  1.73 us

profile of v3, /device:TPU:0, one launch (start us, length us, event | category | flops | bytes accessed | tf_op | source)
XLA Modules:
  0.0 52.2 jit_solution(14235751847233796847)
XLA Ops:
  0.6 49.6 %chebyshev.1 = (bf16[24,64,512]{2,1,0:T(8,128)(2,1)S(1)}, bf16[24,64,512]{2,1,0:T(8,128)(2,1)S(1)}, f32[24,64]{1,0:T(8,128)S(1)}) custom-call(s32[24,25]{1,0:T(8,128)} %mask_h.1, s32[24,128]{1,0:T(8,128)} %owner_h.1, bf16[24,64,512]{2,1,0:T(8,128)(2,1)} %tn.1, bf16[24,64,512]{2,1,0:T(8,128)(2,1)} %tp.1, bf16[24,128,512]{2,1,0:T(8,128)(2,1)} %cot_h.1, ...), custom_call_target="tpu_custom_call" | custom-call | tf_op jit(solution)/shard_map/chebyshev/pallas_call | solution.py:441
  50.3 1.7 %write_out.1 = (bf16[24,64,512]{2,1,0:T(8,128)(2,1)}, bf16[24,64,512]{2,1,0:T(8,128)(2,1)}, f32[24,64]{1,0:T(8,128)}) custom-call(bf16[24,64,512]{2,1,0:T(8,128)(2,1)S(1)} %get-tuple-element.6.a, bf16[24,64,512]{2,1,0:T(8,128)(2,1)S(1)} %get-tuple-element.7.b, f32[24,64]{1,0:T(8,128)S(1)} %get-tuple-element.8.c), custom_call_target="tpu_custom_call" | custom-call | tf_op jit(solution)/shard_map/write_out/pallas_call | solution.py:477

commit v4 on v3

--- a/solution.py
+++ b/solution.py
@@ -31,7 +31,7 @@
 def kernel(
     mask_h, owner_h, tn, tp, cot_h, ham_h, slope_h,
     tno, gro, fo,
-    mask, owner, ext, tt, cot, ham, slope, own, xs, xr, bown, bs, br, prev, to, go, rf, fbuf, fsum,
+    mask, owner, ext, tt, cot, ham, slope, own, xs, xr, bown, bs, br, prev, to, go, rf, fpart, fbuf, fsum,
     lsem, hsem, osem, hs, hr, xss, xrs, bss, bsr, fs, fr,
 ):
     row = lax.axis_index("rows")
@@ -40,10 +40,13 @@
     up = {"rows": lax.rem(row + 1, 16)}
     down = {"rows": lax.rem(row + 15, 16)}
     partner = {"layers": 1 - lay}
-    me = col * 2 + lay
-
-    def ring(index):
-        return {"cols": index // 2, "layers": index % 2}
+    core = lax.rem(col, 2)
+    chip = lay * 2 + lax.div(col, 2)
+    mate = {"cols": col + 1 - 2 * core}
+
+    def ring(o):
+        other = lax.rem(chip + o, 4)
+        return {"cols": lax.rem(other, 2) * 2 + core, "layers": lax.div(other, 2)}
 
     def load_term():
         return pltpu.make_async_copy(tn, ext.at[pl.ds(REACH, ROWS)], lsem.at[0])
@@ -58,10 +61,9 @@
     barrier = pltpu.get_barrier_semaphore()
     pl.semaphore_signal(barrier, 1, device_id=up, device_id_type=MESH)
     pl.semaphore_signal(barrier, 1, device_id=down, device_id_type=MESH)
-    for o in range(1, 8):
-        pl.semaphore_signal(
-            barrier, 1, device_id=ring(lax.rem(me + o, 8)), device_id_type=MESH
-        )
+    pl.semaphore_signal(barrier, 1, device_id=mate, device_id_type=MESH)
+    for o in range(1, 4):
+        pl.semaphore_signal(barrier, 1, device_id=ring(o), device_id_type=MESH)
 
     def load_cot(part):
         at = (pl.ds(10, 4), pl.ds(0, 10), pl.ds(14, 10))[part]
@@ -141,9 +143,8 @@
     with jax.named_scope("rg_term"):
         load_term().wait()
     with jax.named_scope("rg_barrier"):
-        pl.semaphore_wait(barrier, 9)
-    for u in range(3):
-        start_lone(u)
+        pl.semaphore_wait(barrier, 6)
+    start_lone(0)
 
     def turn(pair):
         tt[pair] = ext[pl.ds(2 * pair, 2)].reshape(ORB, COLS).T
@@ -152,14 +153,11 @@
         turn(p + 6)
         return carry
 
-    lax.fori_loop(0, 6, turn_local, 0)
-    start_lone(3)
+    for u in range(1, 4):
+        lax.fori_loop(4 * u - 4, 4 * u, turn_local, 0)
+        start_lone(u)
     for c in load_blocks(1):
         c.start()
-    lax.fori_loop(6, 12, turn_local, 0)
-    start_lone(4)
-    load_cot(1).start()
-    load_cot(2).start()
 
     def mask_rows(k, carry):
         have_blocks(k)
@@ -278,13 +276,16 @@
     with jax.named_scope("rg_mask0"):
         load_mask().wait()
         mask_rows(0, 0)
-    load_cot(0).wait()
+    start_lone(4)
+    load_cot(1).start()
+    load_cot(2).start()
     start_halo(5)
     for k in range(2, STEPS):
         for c in load_blocks(k):
             c.start()
     load_prev().start()
     load_owner().start()
+    load_cot(0).wait()
     with jax.named_scope("rg_fwd0"):
         for u in range(3):
             forward_lone(u)
@@ -318,32 +319,40 @@
     atoms = lax.broadcasted_iota(jnp.int32, (HALF, ORB), 0)
     lanes = lax.broadcasted_iota(jnp.int32, (HALF, ORB), 1)
 
-    def gather_atoms(i, total):
-        mine = jnp.where(owner[pl.ds(i, 1)] == atoms, rf[i], 0.0)
-        summed = jnp.sum(mine, axis=1, keepdims=True)
-        return total + jnp.where(lanes == i, summed, 0.0)
-
-    total = lax.fori_loop(0, ROWS, gather_atoms, jnp.zeros((HALF, ORB), F32))
-    total = jnp.concatenate([total, jnp.zeros((HALF, ORB), F32)], axis=0).T
-    fbuf[me] = total[:ROWS]
+    def gather_atoms(i, totals):
+        both = []
+        for total, j in zip(totals, (i, i + 12)):
+            mine = jnp.where(owner[pl.ds(j, 1)] == atoms, rf[j], 0.0)
+            summed = jnp.sum(mine, axis=1, keepdims=True)
+            both.append(total + jnp.where(lanes == i, summed, 0.0))
+        return tuple(both)
+
+    zero = jnp.zeros((HALF, ORB), F32)
+    totals = lax.fori_loop(0, 12, gather_atoms, (zero, zero))
+    fpart[0] = jnp.concatenate(totals, axis=0).T[:16]
+
+    def to_mate():
+        return remote(fpart.at[0], fpart.at[1], fs.at[0], fr.at[0], mate)
 
     def send_force(o):
-        return remote(
-            fbuf.at[me], fbuf.at[me], fs.at[0], fr.at[0],
-            ring(lax.rem(me + o, 8)),
-        )
+        return remote(fbuf.at[chip], fbuf.at[chip], fs.at[1], fr.at[1], ring(o))
 
     def all_forces():
-        at = pl.ds(0, 7)
-        return remote(fbuf.at[at], fbuf.at[at], fs.at[0], fr.at[0], partner)
-
-    for o in range(1, 8):
+        at = pl.ds(0, 3)
+        return remote(fbuf.at[at], fbuf.at[at], fs.at[1], fr.at[1], partner)
+
+    to_mate().start()
+    with jax.named_scope("rg_push"):
+        bown[0:4] = push_group(3)
+    to_mate().wait()
+    fbuf[chip] = fpart[0] + fpart[1]
+    for o in range(1, 4):
         send_force(o).start()
     for side in range(2):
         send_partial(LAST, side).start()
 
     with jax.named_scope("rg_push"):
-        for g in range(3, 9):
+        for g in range(4, 9):
             bown[4 * (g - 3) : 4 * (g - 2)] = push_group(g)
 
     load_prev().wait()
@@ -401,9 +410,10 @@
     with jax.named_scope("rg_forceW"):
         all_forces().wait_recv()
     summed = fbuf[0]
-    for s in range(1, 8):
+    for s in range(1, 4):
         summed = summed + fbuf[s]
-    fsum[...] = summed[:, :HALF]
+    fsum[0:12] = summed[:12, :HALF]
+    fsum[12:24] = summed[:12, HALF:]
     force_out = pltpu.make_async_copy(fsum, fo, osem.at[2])
     force_out.start()
 
@@ -461,13 +471,14 @@
             pltpu.VMEM(block, BF),
             pltpu.VMEM(block, BF),
             pltpu.VMEM((ROWS, 1, ORB), F32),
-            pltpu.VMEM((8, ROWS, ORB), F32),
+            pltpu.VMEM((2, 16, ORB), F32),
+            pltpu.VMEM((4, 16, ORB), F32),
             pltpu.VMEM((ROWS, HALF), F32),
             dma((6,)), dma((STEPS,)), dma((3,)),
             dma((1,)), dma((LAST + 1,)),
             dma((1,)), dma((LAST + 1,)),
             dma((1,)), dma((3,)),
-            dma((1,)), dma((1,)),
+            dma((2,)), dma((2,)),
         ],
         compiler_params=pltpu.CompilerParams(
             collective_id=0, has_side_effects=True, vmem_limit_bytes=54_000_000

time: 52.3 us -> 51.8 us (level)
  Pallas kernels: 51.4 us -> 50.8 us
    pallas_call x1, Pallas kernels: 49.6 us -> 49.1 us  [local(): pl.pallas_call(kernel, out_shape=tuple((pltpu.VMEM(*s) for s in shapes)),...]
where the time goes in v4:
time: 51.8 us; the launch traced here: 51.6 us
  Pallas kernels  50.8 us (98%)
  between operations  0.8 us (2%)
    pallas_call x1, Pallas kernels, local(): pl.pallas_call(kernel, out_shape=tuple((pltpu.VMEM(*s) for s in shapes)),...  49.1 us
    pallas_call x1, Pallas kernels, local(): pl.pallas_call(write_out, out_shape=tuple((jax.ShapeDtypeStruct(*s) for s...  1.73 us

profile of v4, /device:TPU:0, one launch (start us, length us, event | category | flops | bytes accessed | tf_op | source)
XLA Modules:
  0.0 51.6 jit_solution(15175664994259435427)
XLA Ops:
  0.6 49.1 %chebyshev.1 = (bf16[24,64,512]{2,1,0:T(8,128)(2,1)S(1)}, bf16[24,64,512]{2,1,0:T(8,128)(2,1)S(1)}, f32[24,64]{1,0:T(8,128)S(1)}) custom-call(s32[24,25]{1,0:T(8,128)} %mask_h.1, s32[24,128]{1,0:T(8,128)} %owner_h.1, bf16[24,64,512]{2,1,0:T(8,128)(2,1)} %tn.1, bf16[24,64,512]{2,1,0:T(8,128)(2,1)} %tp.1, bf16[24,128,512]{2,1,0:T(8,128)(2,1)} %cot_h.1, ...), custom_call_target="tpu_custom_call" | custom-call | tf_op jit(solution)/shard_map/chebyshev/pallas_call | solution.py:451
  49.7 1.7 %write_out.1 = (bf16[24,64,512]{2,1,0:T(8,128)(2,1)}, bf16[24,64,512]{2,1,0:T(8,128)(2,1)}, f32[24,64]{1,0:T(8,128)}) custom-call(bf16[24,64,512]{2,1,0:T(8,128)(2,1)S(1)} %get-tuple-element.6.a, bf16[24,64,512]{2,1,0:T(8,128)(2,1)S(1)} %get-tuple-element.7.b, f32[24,64]{1,0:T(8,128)S(1)} %get-tuple-element.8.c), custom_call_target="tpu_custom_call" | custom-call | tf_op jit(solution)/shard_map/write_out/pallas_call | solution.py:488

commit v5 on v4

--- a/solution.py
+++ b/solution.py
@@ -16,7 +16,10 @@
 SLOTS = 25
 REACH = 12
 STEPS = 6
-LONE = ((0, 0, 128), (0, 128, 128), (0, 256, 256), (1, 0, 256), (1, 256, 256))
+LONE = (
+    (0, 0, 128), (0, 128, 128), (0, 256, 128), (0, 384, 128), (1, 0, 256), (1, 256, 256),
+)
+PIECE = 128
 FIRST = len(LONE)
 LAST = FIRST + STEPS - 2
 
@@ -32,7 +35,7 @@
     mask_h, owner_h, tn, tp, cot_h, ham_h, slope_h,
     tno, gro, fo,
     mask, owner, ext, tt, cot, ham, slope, own, xs, xr, bown, bs, br, prev, to, go, rf, fpart, fbuf, fsum,
-    lsem, hsem, osem, hs, hr, xss, xrs, bss, bsr, fs, fr,
+    lsem, hsem, osem, hs, hl, hr, xss, xrs, bss, bsr, fs, fr,
 ):
     row = lax.axis_index("rows")
     col = lax.axis_index("cols")
@@ -94,47 +97,37 @@
         c.start()
     load_cot(0).start()
 
+    near = 1 - lax.div(lax.rem(row, 4), 2)
+
     def to_up(s):
         return remote(
-            ext.at[pl.ds(42 - 2 * s, 2)], ext.at[pl.ds(18 - 2 * s, 2)],
-            hs.at[0], hr.at[s], up,
+            ext.at[pl.ds(44 - 2 * s, 2)], ext.at[pl.ds(20 - 2 * s, 2)],
+            hs.at[0], hr.at[s - FIRST], up,
         )
 
     def to_down(s):
         return remote(
-            ext.at[pl.ds(4 + 2 * s, 2)], ext.at[pl.ds(28 + 2 * s, 2)],
-            hs.at[0], hr.at[s], down,
-        )
-
-    def lone_up(u):
-        away, c0, n = LONE[u]
-        cs = pl.ds(c0, n)
-        return remote(
-            ext.at[pl.ds(35 - away, 1), :, cs], ext.at[pl.ds(11 - away, 1), :, cs],
-            hs.at[0], hr.at[u], up,
-        )
-
-    def lone_down(u):
-        away, c0, n = LONE[u]
-        cs = pl.ds(c0, n)
-        return remote(
-            ext.at[pl.ds(12 + away, 1), :, cs], ext.at[pl.ds(36 + away, 1), :, cs],
-            hs.at[0], hr.at[u], down,
+            ext.at[pl.ds(2 + 2 * s, 2)], ext.at[pl.ds(26 + 2 * s, 2)],
+            hs.at[0], hr.at[s - FIRST], down,
         )
 
     def halo_bytes(rows, cs, sem):
         at = pl.ds(REACH, rows), slice(None), cs
         return remote(ext.at[at], ext.at[at], hs.at[0], sem, up)
 
-    def have_lone(u):
-        halo_bytes(2, pl.ds(LONE[u][1], LONE[u][2]), hr.at[u]).wait_recv()
+    def have_piece(side, h):
+        halo_bytes(2, pl.ds(PIECE * h, PIECE), hl.at[side, h]).wait_recv()
 
     def have_halo(s):
-        halo_bytes(4, pl.ds(0, COLS), hr.at[s]).wait_recv()
-
-    def start_lone(u):
-        lone_up(u).start()
-        lone_down(u).start()
+        halo_bytes(4, pl.ds(0, COLS), hr.at[s - FIRST]).wait_recv()
+
+    def start_piece(h):
+        cs = pl.ds(PIECE * h, PIECE)
+        for side, source, target, device in ((0, 34, 10, up), (1, 12, 36, down)):
+            remote(
+                ext.at[pl.ds(source, 2), :, cs], ext.at[pl.ds(target, 2), :, cs],
+                hs.at[0], hl.at[side, h], device,
+            ).start()
 
     def start_halo(s):
         to_up(s).start()
@@ -144,7 +137,7 @@
         load_term().wait()
     with jax.named_scope("rg_barrier"):
         pl.semaphore_wait(barrier, 6)
-    start_lone(0)
+    start_piece(0)
 
     def turn(pair):
         tt[pair] = ext[pl.ds(2 * pair, 2)].reshape(ORB, COLS).T
@@ -155,7 +148,7 @@
 
     for u in range(1, 4):
         lax.fori_loop(4 * u - 4, 4 * u, turn_local, 0)
-        start_lone(u)
+        start_piece(u)
     for c in load_blocks(1):
         c.start()
 
@@ -171,22 +164,12 @@
         return carry
 
     def step_rows(s, side):
-        return 18 - 2 * s if side == 0 else 4 + 2 * s
+        return 20 - 2 * s if side == 0 else 2 + 2 * s
 
     def send_partial(s, side):
         at = pl.ds(step_rows(s, side), 2)
         return remote(
             xs.at[at], xr.at[at], xss.at[0], xrs.at[s], partner
-        )
-
-    def lone_at(u, side):
-        away, c0, n = LONE[u]
-        return pl.ds(12 + away if side else 11 - away, 1), slice(None), pl.ds(c0, n)
-
-    def send_lone(u, side):
-        at = lone_at(u, side)
-        return remote(
-            xs.at[at], xr.at[at], xss.at[0], xrs.at[u], partner
         )
 
     def stacked(i, before, after):
@@ -216,28 +199,26 @@
             part = 2.0 * jnp.sum(turned * g, axis=0, keepdims=True)
             rf[i] = rf[i] + part if c0 else part
 
-    nothing = jnp.zeros((HALF, COLS), BF)
-
     def forward_lone(u):
-        away, c0, n = LONE[u]
+        other, c0, n = LONE[u]
+        side = 1 - near if other else near
         cs = slice(c0, c0 + n)
         with jax.named_scope("rg_halo"):
-            have_lone(u)
-        low = jnp.concatenate([ext[10, :, cs] if away else nothing[:, :n], ext[11, :, cs]], axis=0)
-        high = jnp.concatenate([ext[36, :, cs], ext[37, :, cs] if away else nothing[:, :n]], axis=0)
-        tt[5, cs] = low.T
-        tt[18, cs] = high.T
-        product(5, 14, ((10, 0), (13, 3)) if away else ((11, 1), (12, 2)), c0, n)
-        for side in range(2):
-            send_lone(u, side).start()
+            for h in range(c0 // PIECE, (c0 + n) // PIECE):
+                have_piece(side, h)
+        tt[5 + 13 * side, cs] = ext[pl.ds(10 + 26 * side, 2), :, cs].reshape(ORB, n).T
+        pair = 5 + side
+        product(pair, 13, ((2 * pair, 0), (2 * pair + 1, 1)), c0, n)
+        at = pl.ds(2 * pair, 2), slice(None), pl.ds(c0, n)
+        remote(xs.at[at], xr.at[at], xss.at[0], xrs.at[u], partner).start()
 
     def forward(s, carry):
         with jax.named_scope("rg_halo"):
             have_halo(s)
-        turn(9 - s)
-        turn(14 + s)
+        turn(10 - s)
+        turn(13 + s)
         for side in range(2):
-            pair = 9 - s if side == 0 else 2 + s
+            pair = 10 - s if side == 0 else 1 + s
             product(pair, 13, ((2 * pair, 0), (2 * pair + 1, 1)))
 
             @pl.when(s < LAST)
@@ -276,10 +257,9 @@
     with jax.named_scope("rg_mask0"):
         load_mask().wait()
         mask_rows(0, 0)
-    start_lone(4)
     load_cot(1).start()
     load_cot(2).start()
-    start_halo(5)
+    start_halo(FIRST)
     for k in range(2, STEPS):
         for c in load_blocks(k):
             c.start()
@@ -287,20 +267,20 @@
     load_owner().start()
     load_cot(0).wait()
     with jax.named_scope("rg_fwd0"):
-        for u in range(3):
+        for u in range(4):
             forward_lone(u)
-    start_halo(6)
+    start_halo(FIRST + 1)
     with jax.named_scope("rg_fwd1"):
-        for u in range(3, 5):
+        for u in range(4, 6):
             forward_lone(u)
-    start_halo(7)
+    start_halo(FIRST + 2)
     with jax.named_scope("rg_mask1"):
         cot_rest().wait()
         mask_rows(1, 0)
-    start_halo(8)
+    start_halo(FIRST + 3)
     with jax.named_scope("rg_fwd2"):
         forward(FIRST, 0)
-    start_halo(9)
+    start_halo(FIRST + 4)
     with jax.named_scope("rg_fwd3"):
         mask_rows(2, 0)
         forward(FIRST + 1, 0)
@@ -433,10 +413,10 @@
 
 def write_out(a, b, c, ao, bo, co, sem):
     copies = [pltpu.make_async_copy(c, co, sem.at[0])]
-    for n, (x, y) in enumerate(((a, ao), (b, bo))):
-        for part in range(4):
-            at = pl.ds(6 * part, 6)
-            copies.append(pltpu.make_async_copy(x.at[at], y.at[at], sem.at[1 + 4 * n + part]))
+    for x, y in ((a, ao), (b, bo)):
+        for part in range(8):
+            at = pl.ds(3 * part, 3)
+            copies.append(pltpu.make_async_copy(x.at[at], y.at[at], sem.at[0]))
     for copy in copies:
         copy.start()
     for copy in copies:
@@ -475,7 +455,7 @@
             pltpu.VMEM((4, 16, ORB), F32),
             pltpu.VMEM((ROWS, HALF), F32),
             dma((6,)), dma((STEPS,)), dma((3,)),
-            dma((1,)), dma((LAST + 1,)),
+            dma((1,)), dma((2, COLS // PIECE)), dma((STEPS - 1,)),
             dma((1,)), dma((LAST + 1,)),
             dma((1,)), dma((3,)),
             dma((2,)), dma((2,)),
@@ -490,7 +470,7 @@
         out_shape=tuple(jax.ShapeDtypeStruct(*s) for s in shapes),
         in_specs=[anyspace] * 3,
         out_specs=(anyspace,) * 3,
-        scratch_shapes=[dma((9,))],
+        scratch_shapes=[dma((1,))],
         compiler_params=pltpu.CompilerParams(vmem_limit_bytes=4_000_000),
         name="write_out",
     )(*results)

time: 51.8 us -> 50.7 us (0.979)
  Pallas kernels: 50.8 us -> 49.8 us
    pallas_call x1, Pallas kernels: 49.1 us -> 48.2 us  [local(): pl.pallas_call(kernel, out_shape=tuple((pltpu.VMEM(*s) for s in shapes)),...]
where the time goes in v5:
time: 50.7 us; the launch traced here: 50.6 us
  Pallas kernels  49.8 us (98%)
  between operations  0.8 us (2%)
    pallas_call x1, Pallas kernels, local(): pl.pallas_call(kernel, out_shape=tuple((pltpu.VMEM(*s) for s in shapes)),...  48.2 us
    pallas_call x1, Pallas kernels, local(): pl.pallas_call(write_out, out_shape=tuple((jax.ShapeDtypeStruct(*s) for s...  1.65 us

profile of v5, /device:TPU:0, one launch (start us, length us, event | category | flops | bytes accessed | tf_op | source)
XLA Modules:
  0.0 50.6 jit_solution(17394145755522798652)
XLA Ops:
  0.6 48.2 %chebyshev.1 = (bf16[24,64,512]{2,1,0:T(8,128)(2,1)S(1)}, bf16[24,64,512]{2,1,0:T(8,128)(2,1)S(1)}, f32[24,64]{1,0:T(8,128)S(1)}) custom-call(s32[24,25]{1,0:T(8,128)} %mask_h.1, s32[24,128]{1,0:T(8,128)} %owner_h.1, bf16[24,64,512]{2,1,0:T(8,128)(2,1)} %tn.1, bf16[24,64,512]{2,1,0:T(8,128)(2,1)} %tp.1, bf16[24,128,512]{2,1,0:T(8,128)(2,1)} %cot_h.1, ...), custom_call_target="tpu_custom_call" | custom-call | tf_op jit(solution)/shard_map/chebyshev/pallas_call | solution.py:431
  48.8 1.7 %write_out.1 = (bf16[24,64,512]{2,1,0:T(8,128)(2,1)}, bf16[24,64,512]{2,1,0:T(8,128)(2,1)}, f32[24,64]{1,0:T(8,128)}) custom-call(bf16[24,64,512]{2,1,0:T(8,128)(2,1)S(1)} %get-tuple-element.6.a, bf16[24,64,512]{2,1,0:T(8,128)(2,1)S(1)} %get-tuple-element.7.b, f32[24,64]{1,0:T(8,128)S(1)} %get-tuple-element.8.c), custom_call_target="tpu_custom_call" | custom-call | tf_op jit(solution)/shard_map/write_out/pallas_call | solution.py:468

commit v6 on v5

--- a/solution.py
+++ b/solution.py
@@ -17,7 +17,8 @@
 REACH = 12
 STEPS = 6
 LONE = (
-    (0, 0, 128), (0, 128, 128), (0, 256, 128), (0, 384, 128), (1, 0, 256), (1, 256, 256),
+    (0, 0, 128), (0, 128, 128), (0, 256, 128), (0, 384, 128),
+    (1, 0, 128), (1, 128, 128), (1, 256, 128), (1, 384, 128),
 )
 PIECE = 128
 FIRST = len(LONE)
@@ -101,13 +102,13 @@
 
     def to_up(s):
         return remote(
-            ext.at[pl.ds(44 - 2 * s, 2)], ext.at[pl.ds(20 - 2 * s, 2)],
+            ext.at[pl.ds(48 - 2 * s, 2)], ext.at[pl.ds(24 - 2 * s, 2)],
             hs.at[0], hr.at[s - FIRST], up,
         )
 
     def to_down(s):
         return remote(
-            ext.at[pl.ds(2 + 2 * s, 2)], ext.at[pl.ds(26 + 2 * s, 2)],
+            ext.at[pl.ds(2 * s - 2, 2)], ext.at[pl.ds(22 + 2 * s, 2)],
             hs.at[0], hr.at[s - FIRST], down,
         )
 
@@ -164,7 +165,7 @@
         return carry
 
     def step_rows(s, side):
-        return 20 - 2 * s if side == 0 else 2 + 2 * s
+        return 24 - 2 * s if side == 0 else 2 * s - 2
 
     def send_partial(s, side):
         at = pl.ds(step_rows(s, side), 2)
@@ -215,10 +216,10 @@
     def forward(s, carry):
         with jax.named_scope("rg_halo"):
             have_halo(s)
-        turn(10 - s)
-        turn(13 + s)
+        turn(12 - s)
+        turn(11 + s)
         for side in range(2):
-            pair = 10 - s if side == 0 else 1 + s
+            pair = 12 - s if side == 0 else s - 1
             product(pair, 13, ((2 * pair, 0), (2 * pair + 1, 1)))
 
             @pl.when(s < LAST)
@@ -271,7 +272,7 @@
             forward_lone(u)
     start_halo(FIRST + 1)
     with jax.named_scope("rg_fwd1"):
-        for u in range(4, 6):
+        for u in range(4, 8):
             forward_lone(u)
     start_halo(FIRST + 2)
     with jax.named_scope("rg_mask1"):

time: 50.7 us -> 50.7 us (level)
  no operation moved by 1% of the time
where the time goes in v6:
time: 50.7 us; the launch traced here: 50.6 us
  Pallas kernels  49.8 us (98%)
  between operations  0.8 us (2%)
    pallas_call x1, Pallas kernels, local(): pl.pallas_call(kernel, out_shape=tuple((pltpu.VMEM(*s) for s in shapes)),...  48.2 us
    pallas_call x1, Pallas kernels, local(): pl.pallas_call(write_out, out_shape=tuple((jax.ShapeDtypeStruct(*s) for s...  1.65 us

profile of v6, /device:TPU:0, one launch (start us, length us, event | category | flops | bytes accessed | tf_op | source)
XLA Modules:
  0.0 50.6 jit_solution(982283361528555280)
XLA Ops:
  0.6 48.2 %chebyshev.1 = (bf16[24,64,512]{2,1,0:T(8,128)(2,1)S(1)}, bf16[24,64,512]{2,1,0:T(8,128)(2,1)S(1)}, f32[24,64]{1,0:T(8,128)S(1)}) custom-call(s32[24,25]{1,0:T(8,128)} %mask_h.1, s32[24,128]{1,0:T(8,128)} %owner_h.1, bf16[24,64,512]{2,1,0:T(8,128)(2,1)} %tn.1, bf16[24,64,512]{2,1,0:T(8,128)(2,1)} %tp.1, bf16[24,128,512]{2,1,0:T(8,128)(2,1)} %cot_h.1, ...), custom_call_target="tpu_custom_call" | custom-call | tf_op jit(solution)/shard_map/chebyshev/pallas_call | solution.py:432
  48.8 1.7 %write_out.1 = (bf16[24,64,512]{2,1,0:T(8,128)(2,1)}, bf16[24,64,512]{2,1,0:T(8,128)(2,1)}, f32[24,64]{1,0:T(8,128)}) custom-call(bf16[24,64,512]{2,1,0:T(8,128)(2,1)S(1)} %get-tuple-element.6.a, bf16[24,64,512]{2,1,0:T(8,128)(2,1)S(1)} %get-tuple-element.7.b, f32[24,64]{1,0:T(8,128)S(1)} %get-tuple-element.8.c), custom_call_target="tpu_custom_call" | custom-call | tf_op jit(solution)/shard_map/write_out/pallas_call | solution.py:469

commit v7 on v6

--- a/solution.py
+++ b/solution.py
@@ -103,13 +103,13 @@
     def to_up(s):
         return remote(
             ext.at[pl.ds(48 - 2 * s, 2)], ext.at[pl.ds(24 - 2 * s, 2)],
-            hs.at[0], hr.at[s - FIRST], up,
+            hs.at[0], hr.at[0, s - FIRST], up,
         )
 
     def to_down(s):
         return remote(
             ext.at[pl.ds(2 * s - 2, 2)], ext.at[pl.ds(22 + 2 * s, 2)],
-            hs.at[0], hr.at[s - FIRST], down,
+            hs.at[0], hr.at[1, s - FIRST], down,
         )
 
     def halo_bytes(rows, cs, sem):
@@ -119,8 +119,8 @@
     def have_piece(side, h):
         halo_bytes(2, pl.ds(PIECE * h, PIECE), hl.at[side, h]).wait_recv()
 
-    def have_halo(s):
-        halo_bytes(4, pl.ds(0, COLS), hr.at[s - FIRST]).wait_recv()
+    def have_halo(side, s):
+        halo_bytes(2, pl.ds(0, COLS), hr.at[side, s - FIRST]).wait_recv()
 
     def start_piece(h):
         cs = pl.ds(PIECE * h, PIECE)
@@ -214,17 +214,17 @@
         remote(xs.at[at], xr.at[at], xss.at[0], xrs.at[u], partner).start()
 
     def forward(s, carry):
-        with jax.named_scope("rg_halo"):
-            have_halo(s)
-        turn(12 - s)
-        turn(11 + s)
-        for side in range(2):
-            pair = 12 - s if side == 0 else s - 1
+        for side in (near, 1 - near):
+            with jax.named_scope("rg_halo"):
+                have_halo(side, s)
+            turn((12 - s) * (1 - side) + (11 + s) * side)
+            pair = (12 - s) * (1 - side) + (s - 1) * side
             product(pair, 13, ((2 * pair, 0), (2 * pair + 1, 1)))
 
             @pl.when(s < LAST)
             def _():
-                send_partial(s, side).start()
+                at = pl.ds(2 * pair, 2)
+                remote(xs.at[at], xr.at[at], xss.at[0], xrs.at[s], partner).start()
 
         return carry
 
@@ -400,7 +400,7 @@
 
     with jax.named_scope("rg_sent"):
         sent = ext.at[pl.ds(0, ROWS)]
-        remote(sent, sent, hs.at[0], hr.at[0], up).wait_send()
+        remote(sent, sent, hs.at[0], hr.at[0, 0], up).wait_send()
         remote(bs, br, bss.at[0], bsr.at[0], up).wait_send()
         all_forces().wait_send()
         force_out.wait()
@@ -456,7 +456,7 @@
             pltpu.VMEM((4, 16, ORB), F32),
             pltpu.VMEM((ROWS, HALF), F32),
             dma((6,)), dma((STEPS,)), dma((3,)),
-            dma((1,)), dma((2, COLS // PIECE)), dma((STEPS - 1,)),
+            dma((1,)), dma((2, COLS // PIECE)), dma((2, STEPS - 1)),
             dma((1,)), dma((LAST + 1,)),
             dma((1,)), dma((3,)),
             dma((2,)), dma((2,)),

time: 50.7 us -> 50.2 us (level)
  no operation moved by 1% of the time
where the time goes in v7:
time: 50.2 us; the launch traced here: 50.1 us
  Pallas kernels  49.3 us (98%)
  between operations  0.8 us (2%)
    pallas_call x1, Pallas kernels, local(): pl.pallas_call(kernel, out_shape=tuple((pltpu.VMEM(*s) for s in shapes)),...  47.7 us
    pallas_call x1, Pallas kernels, local(): pl.pallas_call(write_out, out_shape=tuple((jax.ShapeDtypeStruct(*s) for s...  1.65 us

profile of v7, /device:TPU:0, one launch (start us, length us, event | category | flops | bytes accessed | tf_op | source)
XLA Modules:
  0.0 50.1 jit_solution(3910729037262365161)
XLA Ops:
  0.6 47.7 %chebyshev.1 = (bf16[24,64,512]{2,1,0:T(8,128)(2,1)S(1)}, bf16[24,64,512]{2,1,0:T(8,128)(2,1)S(1)}, f32[24,64]{1,0:T(8,128)S(1)}) custom-call(s32[24,25]{1,0:T(8,128)} %mask_h.1, s32[24,128]{1,0:T(8,128)} %owner_h.1, bf16[24,64,512]{2,1,0:T(8,128)(2,1)} %tn.1, bf16[24,64,512]{2,1,0:T(8,128)(2,1)} %tp.1, bf16[24,128,512]{2,1,0:T(8,128)(2,1)} %cot_h.1, ...), custom_call_target="tpu_custom_call" | custom-call | tf_op jit(solution)/shard_map/chebyshev/pallas_call | solution.py:432
  48.3 1.7 %write_out.1 = (bf16[24,64,512]{2,1,0:T(8,128)(2,1)}, bf16[24,64,512]{2,1,0:T(8,128)(2,1)}, f32[24,64]{1,0:T(8,128)}) custom-call(bf16[24,64,512]{2,1,0:T(8,128)(2,1)S(1)} %get-tuple-element.6.a, bf16[24,64,512]{2,1,0:T(8,128)(2,1)S(1)} %get-tuple-element.7.b, f32[24,64]{1,0:T(8,128)S(1)} %get-tuple-element.8.c), custom_call_target="tpu_custom_call" | custom-call | tf_op jit(solution)/shard_map/write_out/pallas_call | solution.py:469
